TPU v7x, 32 devices: a whole 2x2x4 slice. The times are simulated.
32 devices in a mesh: fsdp: 8 (over y, x, core), tp: 4 (over z).
Axes of the slice: x: 2, y: 2, z: 4, core: 2. Of those that a mesh axis runs over, the one named last changes fastest.
Arguments:
- hidden_in: bfloat16 [2, 8192, 2048], P(None, ('fsdp', 'tp')), may hold values from -27 to 27
- out_grad: bfloat16 [2, 8192, 2048], P(None, ('fsdp', 'tp')), may hold values from -6 to 6
- lengths: int32 [2, 8], P(None, 'fsdp'), may hold values from 256 to 1024, as said below
- qkv_weight: bfloat16 [2048, 6144], P('fsdp', 'tp'), may hold values from -0.125 to 0.125
- qkv_bias: bfloat16 [6144], P(('tp', 'fsdp')), may hold values from -3 to 3
- out_weight: bfloat16 [2048, 2048], P('tp', 'fsdp'), may hold values from -0.5 to 0.5
- out_bias: bfloat16 [2048], P('fsdp'), may hold values from -3 to 3
- fc1_weight: bfloat16 [2048, 8192], P('fsdp', 'tp'), may hold values from -0.125 to 0.125
- fc1_bias: bfloat16 [8192], P(('tp', 'fsdp')), may hold values from -3 to 3
- fc2_weight: bfloat16 [8192, 2048], P('tp', 'fsdp'), may hold values from -0.0625 to 0.0625
- fc2_bias: bfloat16 [2048], P('fsdp'), may hold values from -3 to 3
- ln1_gain: bfloat16 [2048], P('fsdp'), may hold values from 0.5 to 1.5
- ln1_bias: bfloat16 [2048], P('fsdp'), may hold values from -2 to 2
- ln2_gain: bfloat16 [2048], P('fsdp'), may hold values from 0.5 to 1.5
- ln2_bias: bfloat16 [2048], P('fsdp'), may hold values from -2 to 2
Outputs:
- hidden_out: bfloat16 [2, 8192, 2048], P(None, ('fsdp', 'tp'))
- in_grad: bfloat16 [2, 8192, 2048], P(None, ('fsdp', 'tp'))
- grad_qkv_weight: float32 [2048, 6144], P('fsdp', 'tp')
- grad_qkv_bias: float32 [6144], P(('tp', 'fsdp'))
- grad_out_weight: float32 [2048, 2048], P('tp', 'fsdp')
- grad_out_bias: float32 [2048], P('fsdp')
- grad_fc1_weight: float32 [2048, 8192], P('fsdp', 'tp')
- grad_fc1_bias: float32 [8192], P(('tp', 'fsdp'))
- grad_fc2_weight: float32 [8192, 2048], P('tp', 'fsdp')
- grad_fc2_bias: float32 [2048], P('fsdp')
- grad_ln1_gain: float32 [2048], P('fsdp')
- grad_ln1_bias: float32 [2048], P('fsdp')
- grad_ln2_gain: float32 [2048], P('fsdp')
- grad_ln2_bias: float32 [2048], P('fsdp')
Inputs may be any that keep to these rules, and one draw needn't show every extreme that they name: `lengths`: in every micro-batch some slot holds a sequence of 1024 rows.
All inputs are finite; a program needn't handle non-finite values.
Results may differ from a plain program's by a relative error of at most 0.0097.
Values may be sent and summed in bfloat16 or wider, within the bound.
A program may use at most 320 MiB of HBM per device.

v0:
```python
from functools import partial
import math

import jax
import jax.numpy as jnp
from jax import lax
from jax.sharding import PartitionSpec as P

HEAD = 128
ROT = 32


EPSILON = 1e-05
MASKED = -1e30


def layer_norm(row_block, norm_gain, norm_shift):
    row_mean = jnp.mean(row_block, axis=-1, keepdims=True)
    centred = row_block - row_mean
    spread = jnp.mean(centred * centred, axis=-1, keepdims=True)
    return centred * lax.rsqrt(spread + EPSILON) * norm_gain + norm_shift


def layer_norm_pair(row_block, gain_first, shift_first, gain_second, shift_second):
    return (
        layer_norm(row_block, gain_first, shift_first),
        layer_norm(row_block, gain_second, shift_second),
    )


def rotary_tables(row_count, rot_width):
    exponent = jnp.arange(0, rot_width, 2).astype(jnp.float32) / rot_width
    inverse = 1.0 / 10000.0**exponent
    places = jnp.arange(row_count).astype(jnp.float32)
    angles = places[:, None] * inverse[None, :]
    angles = jnp.concatenate([angles, angles], axis=-1)
    return (jnp.cos(angles)[:, None, :], jnp.sin(angles)[:, None, :])


def rotate(head_block, cosine_table, sine_table, rot_width):
    half_width = rot_width // 2
    turning = head_block[..., :rot_width]
    turned = jnp.concatenate([-turning[..., half_width:], turning[..., :half_width]], axis=-1)
    return jnp.concatenate(
        [turning * cosine_table + turned * sine_table, head_block[..., rot_width:]], axis=-1
    )


def unrotate(head_block, cosine_table, sine_table, rot_width):
    half_width = rot_width // 2
    turning = head_block[..., :rot_width]
    scaled = turning * sine_table
    turned_back = jnp.concatenate([scaled[..., half_width:], -scaled[..., :half_width]], axis=-1)
    return jnp.concatenate(
        [turning * cosine_table + turned_back, head_block[..., rot_width:]], axis=-1
    )


def inner_rows(first_arr, second_arr):
    return lax.dot_general(
        first_arr, second_arr, (((0,), (0,)), ((), ())), preferred_element_type=jnp.float32
    )


def times_transposed(first_arr, second_arr):
    return lax.dot_general(
        first_arr, second_arr, (((1,), (1,)), ((), ())), preferred_element_type=jnp.float32
    )


def fetch_weights(
    qkv_weight,
    qkv_bias,
    out_weight,
    out_bias,
    fc1_weight,
    fc1_bias,
    fc2_weight,
    fc2_bias,
    ln1_gain,
    ln1_bias,
    ln2_gain,
    ln2_bias,
):
    return (
        lax.all_gather(qkv_weight, "fsdp", axis=0, tiled=True),
        lax.all_gather(qkv_bias, "fsdp", axis=0, tiled=True),
        lax.all_gather(out_weight, "fsdp", axis=1, tiled=True),
        lax.all_gather(out_bias, "fsdp", axis=0, tiled=True),
        lax.all_gather(fc1_weight, "fsdp", axis=0, tiled=True),
        lax.all_gather(fc1_bias, "fsdp", axis=0, tiled=True),
        lax.all_gather(fc2_weight, "fsdp", axis=1, tiled=True),
        lax.all_gather(fc2_bias, "fsdp", axis=0, tiled=True),
        lax.all_gather(ln1_gain, "fsdp", axis=0, tiled=True),
        lax.all_gather(ln1_bias, "fsdp", axis=0, tiled=True),
        lax.all_gather(ln2_gain, "fsdp", axis=0, tiled=True),
        lax.all_gather(ln2_bias, "fsdp", axis=0, tiled=True),
    )


def reduce_grads(grad_set):
    summed = (
        lax.psum_scatter(grad_set[0], "fsdp", scatter_dimension=0, tiled=True),
        lax.psum_scatter(grad_set[1], "fsdp", scatter_dimension=0, tiled=True),
        lax.psum_scatter(grad_set[2], "fsdp", scatter_dimension=1, tiled=True),
        lax.psum_scatter(grad_set[3], "fsdp", scatter_dimension=0, tiled=True),
        lax.psum_scatter(grad_set[4], "fsdp", scatter_dimension=0, tiled=True),
        lax.psum_scatter(grad_set[5], "fsdp", scatter_dimension=0, tiled=True),
        lax.psum_scatter(grad_set[6], "fsdp", scatter_dimension=1, tiled=True),
        lax.psum_scatter(grad_set[7], "fsdp", scatter_dimension=0, tiled=True),
        lax.psum_scatter(grad_set[8], "fsdp", scatter_dimension=0, tiled=True),
        lax.psum_scatter(grad_set[9], "fsdp", scatter_dimension=0, tiled=True),
        lax.psum_scatter(grad_set[10], "fsdp", scatter_dimension=0, tiled=True),
        lax.psum_scatter(grad_set[11], "fsdp", scatter_dimension=0, tiled=True),
    )
    norm_sums = lax.psum((summed[8], summed[9], summed[10], summed[11]), "tp")
    return tuple(summed[:8]) + tuple(norm_sums)


def add_grads(earlier, later):
    if earlier is None:
        return tuple(later)
    return tuple(jax.tree.map(jnp.add, tuple(earlier), tuple(later)))


def shards(
    hidden_in,
    out_grad,
    lengths,
    qkv_weight,
    qkv_bias,
    out_weight,
    out_bias,
    fc1_weight,
    fc1_bias,
    fc2_weight,
    fc2_bias,
    ln1_gain,
    ln1_bias,
    ln2_gain,
    ln2_bias,
):
    tp_size = lax.axis_size("tp")
    tp_index = lax.axis_index("tp")
    micro_count, shard_rows, model_width = hidden_in.shape
    slot_rows = shard_rows * tp_size
    block_rows = min(512, slot_rows)
    block_count = slot_rows // block_rows
    score_scale = 1.0 / math.sqrt(HEAD)
    cosine_table, sine_table = rotary_tables(slot_rows, ROT)
    row_ids = jnp.arange(slot_rows)
    shard_ids = tp_index * shard_rows + jnp.arange(shard_rows)
    outputs = []
    in_grads = []
    grad_accum = None
    totals = None
    for micro_step in range(micro_count):
        gathered = fetch_weights(
            qkv_weight,
            qkv_bias,
            out_weight,
            out_bias,
            fc1_weight,
            fc1_bias,
            fc2_weight,
            fc2_bias,
            ln1_gain,
            ln1_bias,
            ln2_gain,
            ln2_bias,
        )
        qkv_mat, qkv_add, out_mat, out_add, up_mat, up_add, down_mat, down_add = gathered[:8]
        gain_one = gathered[8].astype(jnp.float32)
        shift_one = gathered[9].astype(jnp.float32)
        gain_two = gathered[10].astype(jnp.float32)
        shift_two = gathered[11].astype(jnp.float32)
        length = lengths[micro_step, 0]
        valid_full = (row_ids < length).astype(jnp.float32)[:, None]
        valid_shard = (shard_ids < length).astype(jnp.float32)[:, None]
        local_rows = hidden_in[micro_step].astype(jnp.float32)
        normed_one = layer_norm(local_rows, gain_one, shift_one).astype(jnp.bfloat16)
        normed_two = layer_norm(local_rows, gain_two, shift_two).astype(jnp.bfloat16)
        normed_one, normed_two, cot_full = (
            lax.all_gather(normed_one, "tp", axis=0, tiled=True),
            lax.all_gather(normed_two, "tp", axis=0, tiled=True),
            lax.all_gather(out_grad[micro_step], "tp", axis=0, tiled=True),
        )
        heads_here = qkv_mat.shape[1] // (3 * HEAD)
        projected = jnp.dot(
            normed_one, qkv_mat, preferred_element_type=jnp.float32
        ) + qkv_add.astype(jnp.float32)
        projected = projected.reshape(slot_rows, heads_here, 3, HEAD)
        queries = rotate(projected[:, :, 0], cosine_table, sine_table, ROT).astype(jnp.bfloat16)
        keys_all = rotate(projected[:, :, 1], cosine_table, sine_table, ROT).astype(jnp.bfloat16)
        values_all = projected[:, :, 2].astype(jnp.bfloat16)

        def score_block(start_row):
            query_block = lax.dynamic_slice_in_dim(queries, start_row, block_rows, 0)
            scores = (
                jnp.einsum(
                    "qhd,khd->hqk", query_block, keys_all, preferred_element_type=jnp.float32
                )
                * score_scale
            )
            query_rows = start_row + jnp.arange(block_rows)
            allowed = (row_ids[None, :] <= query_rows[:, None]) & (row_ids[None, :] < length)
            return (query_block, jnp.where(allowed[None], scores, MASKED))

        def attend_block(block_idx):
            query_block, scores = score_block(block_idx * block_rows)
            row_top = jnp.max(scores, axis=-1, keepdims=True)
            raised = jnp.exp(scores - row_top)
            row_total = jnp.sum(raised, axis=-1, keepdims=True)
            prob_rows = (raised / row_total).astype(jnp.bfloat16)
            mixed_rows = jnp.einsum(
                "hqk,khd->qhd", prob_rows, values_all, preferred_element_type=jnp.float32
            )
            return (mixed_rows.astype(jnp.bfloat16), (row_top + jnp.log(row_total))[..., 0])

        attended, log_totals = lax.map(attend_block, jnp.arange(block_count))
        attended = attended.reshape(slot_rows, heads_here * HEAD)
        pre_act = jnp.dot(normed_two, up_mat, preferred_element_type=jnp.float32) + up_add.astype(
            jnp.float32
        )
        activated = jax.nn.gelu(pre_act, approximate=False).astype(jnp.bfloat16)
        branch_sum = lax.psum_scatter(
            jnp.dot(attended, out_mat, preferred_element_type=jnp.float32)
            + jnp.dot(activated, down_mat, preferred_element_type=jnp.float32),
            "tp",
            scatter_dimension=0,
            tiled=True,
        )
        result = (
            local_rows + branch_sum + out_add.astype(jnp.float32) + down_add.astype(jnp.float32)
        )
        outputs.append((valid_shard * result).astype(jnp.bfloat16))
        cot_rows = (cot_full.astype(jnp.float32) * valid_full).astype(jnp.bfloat16)
        cot_sum = jnp.sum(cot_rows, axis=0, dtype=jnp.float32)
        grad_out_mat = inner_rows(attended, cot_rows)
        grad_down_mat = inner_rows(activated, cot_rows)
        grad_attended = times_transposed(cot_rows, out_mat).astype(jnp.bfloat16)
        grad_activated = times_transposed(cot_rows, down_mat)
        primal_gelu, gelu_back = jax.vjp(partial(jax.nn.gelu, approximate=False), pre_act)
        grad_pre = gelu_back(grad_activated)[0].astype(jnp.bfloat16)
        grad_up_mat = inner_rows(normed_two, grad_pre)
        grad_up_add = jnp.sum(grad_pre, axis=0, dtype=jnp.float32)
        grad_mixed = grad_attended.reshape(slot_rows, heads_here, HEAD)

        def back_block(running, scanned):
            grad_keys, grad_values = running
            block_idx, log_total = scanned
            start_row = block_idx * block_rows
            query_block, scores = score_block(start_row)
            prob_rows = jnp.exp(scores - log_total[..., None])
            grad_block = lax.dynamic_slice_in_dim(grad_mixed, start_row, block_rows, 0)
            grad_probs = jnp.einsum(
                "qhd,khd->hqk", grad_block, values_all, preferred_element_type=jnp.float32
            )
            row_dot = jnp.sum(prob_rows * grad_probs, axis=-1, keepdims=True)
            grad_scores = (prob_rows * (grad_probs - row_dot)).astype(jnp.bfloat16)
            grad_query = (
                jnp.einsum(
                    "hqk,khd->qhd", grad_scores, keys_all, preferred_element_type=jnp.float32
                )
                * score_scale
            )
            grad_keys = (
                grad_keys
                + jnp.einsum(
                    "hqk,qhd->khd", grad_scores, query_block, preferred_element_type=jnp.float32
                )
                * score_scale
            )
            grad_values = grad_values + jnp.einsum(
                "hqk,qhd->khd",
                prob_rows.astype(jnp.bfloat16),
                grad_block,
                preferred_element_type=jnp.float32,
            )
            return ((grad_keys, grad_values), grad_query)

        zero_rows = jnp.zeros((slot_rows, heads_here, HEAD), jnp.float32)
        (grad_keys, grad_values), grad_queries = lax.scan(
            back_block, (zero_rows, zero_rows), (jnp.arange(block_count), log_totals)
        )
        grad_queries = grad_queries.reshape(slot_rows, heads_here, HEAD)
        grad_projected = jnp.stack(
            [
                unrotate(grad_queries, cosine_table, sine_table, ROT),
                unrotate(grad_keys, cosine_table, sine_table, ROT),
                grad_values,
            ],
            axis=2,
        )
        grad_projected = grad_projected.reshape(slot_rows, 3 * heads_here * HEAD).astype(
            jnp.bfloat16
        )
        grad_qkv_mat = inner_rows(normed_one, grad_projected)
        grad_qkv_add = jnp.sum(grad_projected, axis=0, dtype=jnp.float32)
        norm_grads = lax.psum_scatter(
            jnp.concatenate(
                [times_transposed(grad_projected, qkv_mat), times_transposed(grad_pre, up_mat)],
                axis=-1,
            ),
            "tp",
            scatter_dimension=0,
            tiled=True,
        )
        primal_norms, norm_back = jax.vjp(
            layer_norm_pair, local_rows, gain_one, shift_one, gain_two, shift_two
        )
        grad_rows, grad_gain_one, grad_shift_one, grad_gain_two, grad_shift_two = norm_back(
            (norm_grads[:, :model_width], norm_grads[:, model_width:])
        )
        residual_grad = valid_shard * out_grad[micro_step].astype(jnp.float32)
        in_grads.append((grad_rows + residual_grad).astype(jnp.bfloat16))
        micro_grads = (
            grad_qkv_mat,
            grad_qkv_add,
            grad_out_mat,
            cot_sum,
            grad_up_mat,
            grad_up_add,
            grad_down_mat,
            cot_sum,
            grad_gain_one,
            grad_shift_one,
            grad_gain_two,
            grad_shift_two,
        )
        grad_accum = add_grads(grad_accum, micro_grads)
    totals = reduce_grads(grad_accum)
    return (
        jnp.stack(outputs),
        jnp.stack(in_grads),
        totals[0],
        totals[1],
        totals[2],
        totals[3],
        totals[4],
        totals[5],
        totals[6],
        totals[7],
        totals[8],
        totals[9],
        totals[10],
        totals[11],
    )


def solution(mesh):
    return jax.shard_map(
        shards,
        mesh=mesh,
        in_specs=(
            P(None, ("fsdp", "tp"), None),
            P(None, ("fsdp", "tp"), None),
            P(None, "fsdp"),
            P("fsdp", "tp"),
            P(("tp", "fsdp")),
            P("tp", "fsdp"),
            P("fsdp"),
            P("fsdp", "tp"),
            P(("tp", "fsdp")),
            P("tp", "fsdp"),
            P("fsdp"),
            P("fsdp"),
            P("fsdp"),
            P("fsdp"),
            P("fsdp"),
        ),
        out_specs=(
            P(None, ("fsdp", "tp"), None),
            P(None, ("fsdp", "tp"), None),
            P("fsdp", "tp"),
            P(("tp", "fsdp")),
            P("tp", "fsdp"),
            P("fsdp"),
            P("fsdp", "tp"),
            P(("tp", "fsdp")),
            P("tp", "fsdp"),
            P("fsdp"),
            P("fsdp"),
            P("fsdp"),
            P("fsdp"),
            P("fsdp"),
        ),
        check_vma=False,
    )
```

profile of v0, /device:TPU:0, one launch (start us, length us, event | category | flops | bytes accessed | tf_op | source)
XLA Modules:
  0.0 1966.9 jit_solution(5079000807032105731)
XLA Ops:
  60.9 14.0 all-reduce
  83.8 39.5 %all-gather.38.cloned.1.call-done = bf16[1,1024,2048]{2,1,0:T(8,128)(2,1)} async-done(((bf16[1,256,2048]{2,1,0:T(8,128)(2,1)}), bf16[1,1024,2048]{2,1,0:T(8,128)(2,1)}) %all-gather.38.cloned.1.call-update) | async-done | bytes 4194320 | tf_op jit(solution)/shard_map/all_gather | solution.py:186
  129.5 74.6 %all-gather.36.cloned.1.call-done = bf16[1,1024,2048]{2,1,0:T(8,128)(2,1)} async-done(((bf16[1,256,2048]{2,1,0:T(8,128)(2,1)}), bf16[1,1024,2048]{2,1,0:T(8,128)(2,1)}) %all-gather.36.cloned.1.call-update) | async-done | bytes 4194320 | tf_op jit(solution)/shard_map/all_gather | solution.py:186
  209.8 75.7 %all-gather.32.cloned.1.call-done = bf16[1024,2048]{1,0:T(8,128)(2,1)} async-done(((bf16[256,2048]{1,0:T(8,128)(2,1)}), bf16[1024,2048]{1,0:T(8,128)(2,1)}) %all-gather.32.cloned.1.call-update) | async-done | bytes 4194320 | tf_op jit(solution)/shard_map/all_gather | solution.py:184
  285.5 45.8 %all-gather.22.cloned.1.call-done = bf16[2048,1536]{1,0:T(8,128)(2,1)} async-done(((bf16[256,1536]{1,0:T(8,128)(2,1)}), bf16[2048,1536]{1,0:T(8,128)(2,1)}) %all-gather.22.cloned.1.call-update) | async-done | bytes 6291472 | tf_op jit(solution)/shard_map/all_gather | solution.py:86
  359.6 53.9 %all-gather.20.cloned.1.call-done = bf16[1024,2048]{1,0:T(8,128)(2,1)} async-done(((bf16[256,2048]{1,0:T(8,128)(2,1)}), bf16[1024,2048]{1,0:T(8,128)(2,1)}) %all-gather.20.cloned.1.call-update) | async-done | bytes 4194320 | tf_op jit(solution)/shard_map/all_gather | solution.py:184
  447.8 22.6 %while.61 = (s32[]{:T(128)}, bf16[2,512,4,128]{3,2,1,0:T(4,128)(2,1)}, f32[2,4,512]{2,1,0:T(4,128)S(1)}, s32[2]{0:T(128)S(1)}, s32[]{:T(128)}, /*index=5*/bf16[1...) while((s32[]{:T(128)}, ...), condition=%wide.region_12.13_spmd.clone.clone, body=%wide.region_9.12_spmd.clone.clone.sunk | while | flops 1100217856 | bytes 39917828 | solution.py:220
  494.4 54.8 %all-gather.28.cloned.1.call-done = bf16[2048,2048]{1,0:T(8,128)(2,1)} async-done(((bf16[256,2048]{1,0:T(8,128)(2,1)}), bf16[2048,2048]{1,0:T(8,128)(2,1)}) %all-gather.28.cloned.1.call-update) | async-done | bytes 8388624 | tf_op jit(solution)/shard_map/all_gather | solution.py:90
  549.3 14.5 fusion.203
  563.8 68.4 %all-gather.26.cloned.1.call-done = bf16[1024,2048]{1,0:T(8,128)(2,1)} async-done(((bf16[256,2048]{1,0:T(8,128)(2,1)}), bf16[1024,2048]{1,0:T(8,128)(2,1)}) %all-gather.26.cloned.1.call-update) | async-done | bytes 4194320 | tf_op jit(solution)/shard_map/all_gather | solution.py:185
  632.2 49.9 %multiply_convert_fusion.3 = (bf16[1024,2048]{1,0:T(8,128)(2,1)}, f32[1024,2048]{1,0:T(8,128)}, bf16[1024,2048]{1,0:T(8,128)(2,1)}, f32[1024,2048]{1,0:T(8,128)}, f32[1024,2048]{1,0:T(8,128)}) fusion(f32[2048]{0:T(1024)S(1)} %bitcast.416, f32[1024,2048]{1,0:T(8,128)} %fusion.203, bf16[1024,2048]{1,0:T(8,128)(2,1)} %all-gather.26.cloned.1.call-done, ...), kind=kOutput, calls=%fused_computation.133 | convolution fusion | flops 8866758656 | bytes 54534144 | tf_op jit(solution)/shard_map/dot_general | solution.py:222
  708.1 24.5 %while.60 = (s32[]{:T(128)}, bf16[2,512,4,128]{3,2,1,0:T(4,128)(2,1)}, f32[2,4,512]{2,1,0:T(4,128)S(1)}, s32[2]{0:T(128)S(1)}, s32[]{:T(128)}, /*index=5*/bf16[1...) while((s32[]{:T(128)}, ...), condition=%wide.region_5.6_spmd.clone.clone, body=%wide.region_2.5_spmd.clone.clone.sunk | while | flops 1100217856 | bytes 44112156 | solution.py:220
  732.6 85.5 %while.62 = (s32[]{:T(128)}, f32[1024,4,128]{0,2,1:T(8,128)S(1)}, f32[1024,4,128]{0,2,1:T(8,128)}, f32[2,512,4,128]{1,0,3,2:T(2,128)}, s32[2]{0:T(128)S(1)}, /*i...) while((s32[]{:T(128)}, f32[1024,4,128]{0,2,1:T(8,128)S(1)}, ...), condition=%wide.region_16.17_spmd.clone.clone, body=%wide.region_14.16_spmd.clone.clone.sunk | while | flops 2719743488 | bytes 96532816 | solution.py:283
  755.2 19.7 dynamic_update_slice.48
  798.4 19.7 dynamic_update_slice.48
  822.8 12.8 fusion.202
  843.2 39.6 %while.63 = (s32[]{:T(128)}, f32[1024,4,128]{0,2,1:T(8,128)S(1)}, f32[1024,4,128]{0,2,1:T(8,128)}, f32[2,512,4,128]{3,1,0,2:T(8,128)}, s32[2]{0:T(128)S(1)}, /*i...) while((s32[]{:T(128)}, f32[1024,4,128]{0,2,1:T(8,128)S(1)}, ...), condition=%wide.region_24.25_spmd.clone.clone, body=%wide.region_22.24_spmd.clone.clone.sunk | while | flops 2719743488 | bytes 109115784 | solution.py:283
  920.9 19.5 convert_reduce_fusion
  940.5 12.8 fusion.208
  975.3 19.4 convert_reduce_fusion.1
  1024.6 12.7 fusion.209
  1037.3 13.1 convolution_add_fusion
  1050.9 15.5 fusion.210
  1066.4 16.2 convolution_add_fusion.2
  1082.9 15.8 fusion.178
  1098.7 16.5 convolution_add_fusion.1
  1139.7 142.5 %reduce-scatter.15.cloned.1.call-done = f32[256,4096]{1,0:T(8,128)} async-done(((f32[1024,4096]{1,0:T(8,128)}), f32[256,4096]{1,0:T(8,128)}) %reduce-scatter.15.cloned.1.call-update) | async-done | bytes 4194320 | tf_op jit(solution)/shard_map/reduce_scatter | solution.py:300
  1282.2 283.4 %reduce-scatter.13.cloned.1.call-done = f32[256,4096]{1,0:T(8,128)} async-done(((f32[1024,4096]{1,0:T(8,128)}), f32[256,4096]{1,0:T(8,128)}) %reduce-scatter.13.cloned.1.call-update) | async-done | bytes 4194320 | tf_op jit(solution)/shard_map/reduce_scatter | solution.py:300
  1577.3 24.8 %all-reduce.8 = (f32[1536]{0:T(1024)S(1)}, f32[2048]{0:T(1024)S(1)}, f32[2048]{0:T(1024)S(1)}, f32[2048]{0:T(1024)S(1)}, f32[2048]{0:T(1024)S(1)}, /*index=5*/f32[2048]{0:T(1024)S(1)}, f32[2048]{0:T(1024)S(1)}) all-reduce(f32[1536]{0:T(1024)S(1)} %add.391, f32[2048]{0:T(1024)S(1)} %add.393, ...), channel_id=9, replica_groups=mesh['fsdp'=8,'tp'=4] {'fsdp'}, use_global_device_ids=true, to_apply=%region_33.34.clone | all-reduce | flops 13824 | bytes 110592
  1625.1 93.4 %reduce-scatter.17.cloned.1.call-done = f32[256,1536]{1,0:T(8,128)} async-done(((f32[2048,1536]{1,0:T(8,128)}), f32[256,1536]{1,0:T(8,128)}) %reduce-scatter.17.cloned.1.call-update) | async-done | bytes 1572880 | tf_op jit(solution)/shard_map/reduce_scatter | solution.py:103
  1718.5 120.4 %reduce-scatter.21.cloned.1.call-done = f32[256,2048]{1,0:T(8,128)} async-done(((f32[2048,2048]{1,0:T(8,128)}), f32[256,2048]{1,0:T(8,128)}) %reduce-scatter.21.cloned.1.call-update) | async-done | bytes 2097168 | tf_op jit(solution)/shard_map/reduce_scatter | solution.py:107
  1838.9 120.4 %reduce-scatter.23.cloned.1.call-done = f32[2048,256]{1,0:T(8,128)} async-done(((f32[2048,2048]{1,0:T(8,128)}), f32[2048,256]{1,0:T(8,128)}) %reduce-scatter.23.cloned.1.call-update) | async-done | bytes 2097168 | tf_op jit(solution)/shard_map/reduce_scatter | solution.py:109
  (509 shorter events, 472.7 us)
Async XLA Ops:
  7.2 40.9 %copy-start.9 = (bf16[2,256,2048]{2,1,0:T(8,128)(2,1)S(1)}, bf16[2,256,2048]{2,1,0:T(8,128)(2,1)}, u32[]{:S(2)}) copy-start(bf16[2,256,2048]{2,1,0:T(8,128)(2,1)} %param.23) | copy-start | bytes 6291460
  7.2 76.5 %all-gather.24.cloned.1.call-start = ((), (), s32[]{:S(2)}) async-start(), calls=%async_computation.10 | async-start | bytes 2359296 | tf_op jit(solution)/shard_map/all_gather | solution.py:88
  8.0 115.3 %all-gather.38.cloned.1.call-start = ((), (), s32[]{:S(2)}) async-start(), calls=%async_computation.25 | async-start | bytes 5242880 | tf_op jit(solution)/shard_map/all_gather | solution.py:186
  11.2 193.0 %all-gather.36.cloned.1.call-start = ((), (), s32[]{:S(2)}) async-start(), calls=%async_computation.24 | async-start | bytes 5242880 | tf_op jit(solution)/shard_map/all_gather | solution.py:186
  11.9 273.6 %all-gather.32.cloned.1.call-start = ((), (), s32[]{:S(2)}) async-start(), calls=%async_computation.15 | async-start | bytes 5242880 | tf_op jit(solution)/shard_map/all_gather | solution.py:184
  53.3 278.0 %all-gather.22.cloned.1.call-start = ((), (), s32[]{:S(2)}) async-start(), calls=%async_computation.9 | async-start | bytes 7077888 | tf_op jit(solution)/shard_map/all_gather | solution.py:86
  53.8 359.7 %all-gather.20.cloned.1.call-start = ((), (), s32[]{:S(2)}) async-start(), calls=%async_computation.8 | async-start | bytes 5242880 | tf_op jit(solution)/shard_map/all_gather | solution.py:184
  54.4 440.0 %all-gather.34.cloned.1.call-start = ((), (), s32[]{:S(2)}) async-start(), calls=%async_computation.16 | async-start | bytes 5242880 | tf_op jit(solution)/shard_map/all_gather | solution.py:185
  55.2 494.1 %all-gather.28.cloned.1.call-start = ((), (), s32[]{:S(2)}) async-start(), calls=%async_computation.12 | async-start | bytes 9437184 | tf_op jit(solution)/shard_map/all_gather | solution.py:90
  55.9 576.3 %all-gather.26.cloned.1.call-start = ((), (), s32[]{:S(2)}) async-start(), calls=%async_computation.11 | async-start | bytes 5242880 | tf_op jit(solution)/shard_map/all_gather | solution.py:185
  56.7 631.8 %all-gather.30.cloned.1.call-start = ((), (), s32[]{:S(2)}) async-start(), calls=%async_computation.13 | async-start | bytes 9437184 | tf_op jit(solution)/shard_map/all_gather | solution.py:92
  57.2 1082.5 %reduce-scatter.11.cloned.1.call-start = ((), (), s32[]{:S(2)}) async-start(), calls=%async_computation.17 | async-start | bytes 10485760 | tf_op jit(solution)/shard_map/reduce_scatter | solution.py:226
  58.7 145.5 %copy-start.72 = (f32[1024]{0:T(1024)}, f32[1024]{0:T(1024)S(1)}, u32[]{:S(2)}) copy-start(f32[1024]{0:T(1024)S(1)} %fusion.170) | copy-start | bytes 12292
  59.3 70.2 %copy-start.64 = (f32[1024]{0:T(1024)}, f32[1024]{0:T(1024)S(1)}, u32[]{:S(2)}) copy-start(f32[1024]{0:T(1024)S(1)} %fusion.171) | copy-start | bytes 12292
  83.7 354.6 %copy-start.50 = (f32[1024,32]{0,1:T(8,128)}, f32[1024,32]{0,1:T(8,128)S(1)}, u32[]{:S(2)}) copy-start(f32[1024,32]{0,1:T(8,128)S(1)} %get-tuple-element.766) | copy-start | bytes 393220
  83.7 354.6 %copy-start.52 = (f32[1024,32]{0,1:T(8,128)}, f32[1024,32]{0,1:T(8,128)S(1)}, u32[]{:S(2)}) copy-start(f32[1024,32]{0,1:T(8,128)S(1)} %get-tuple-element.765) | copy-start | bytes 393220
  83.7 120.4 %copy-start.25 = (bf16[512,2048]{1,0:T(8,128)(2,1)S(1)}, bf16[512,2048]{1,0:T(8,128)(2,1)}, u32[]{:S(2)}) copy-start(bf16[512,2048]{1,0:T(8,128)(2,1)} %all-gather.24.cloned.1.call-done) | copy-start | bytes 6291460
  488.5 143.7 %copy-start.84 = (f32[8,1,256]{2,1,0:T(1,128)S(1)}, f32[8,1,256]{2,1,0:T(1,128)}, u32[]{:S(2)}) copy-start(f32[8,1,256]{2,1,0:T(1,128)} %convert_element_type.294) | copy-start | bytes 24580
  706.7 433.0 %reduce-scatter.9.cloned.1.call-start = ((), (), s32[]{:S(2)}) async-start(), calls=%async_computation.14 | async-start | bytes 10485760 | tf_op jit(solution)/shard_map/reduce_scatter | solution.py:226
  708.1 24.5 %copy-start.1 = (f32[1024,4,128]{0,2,1:T(8,128)S(1)}, f32[1024,4,128]{0,2,1:T(8,128)}, u32[]{:S(2)}) copy-start(f32[1024,4,128]{0,2,1:T(8,128)} %custom-call) | copy-start | bytes 6291460
  841.4 440.8 %reduce-scatter.15.cloned.1.call-start = ((), (), s32[]{:S(2)}) async-start(), calls=%async_computation.19 | async-start | bytes 20971520 | tf_op jit(solution)/shard_map/reduce_scatter | solution.py:300
  959.4 606.2 %reduce-scatter.13.cloned.1.call-start = ((), (), s32[]{:S(2)}) async-start(), calls=%async_computation.18 | async-start | bytes 20971520 | tf_op jit(solution)/shard_map/reduce_scatter | solution.py:300
  1013.5 611.6 %reduce-scatter.19.cloned.1.call-start = ((), (), s32[]{:S(2)}) async-start(), calls=%async_computation.21 | async-start | bytes 4718592 | tf_op jit(solution)/shard_map/reduce_scatter | solution.py:105
  1024.5 694.0 %reduce-scatter.17.cloned.1.call-start = ((), (), s32[]{:S(2)}) async-start(), calls=%async_computation.20 | async-start | bytes 14155776 | tf_op jit(solution)/shard_map/reduce_scatter | solution.py:103
  1050.5 788.4 %reduce-scatter.21.cloned.1.call-start = ((), (), s32[]{:S(2)}) async-start(), calls=%async_computation.22 | async-start | bytes 18874368 | tf_op jit(solution)/shard_map/reduce_scatter | solution.py:107
  1082.7 876.6 %reduce-scatter.23.cloned.1.call-start = ((), (), s32[]{:S(2)}) async-start(), calls=%async_computation.23 | async-start | bytes 18874368 | tf_op jit(solution)/shard_map/reduce_scatter | solution.py:109
  1135.4 430.3 %copy-start.10 = (bf16[2,256,2048]{2,1,0:T(8,128)(2,1)S(1)}, bf16[2,256,2048]{2,1,0:T(8,128)(2,1)}, u32[]{:S(2)}) copy-start(bf16[2,256,2048]{2,1,0:T(8,128)(2,1)} %param.23) | copy-start | bytes 6291460
  1135.4 430.3 %copy-start.59 = (f32[8,1,256]{2,1,0:T(1,128)S(1)}, f32[8,1,256]{2,1,0:T(1,128)}, u32[]{:S(2)}) copy-start(f32[8,1,256]{2,1,0:T(1,128)} %copy-done.58) | copy-start | bytes 24580
  1135.4 430.3 %copy-start.61 = (f32[8,1,256]{2,1,0:T(1,128)S(1)}, f32[8,1,256]{2,1,0:T(1,128)}, u32[]{:S(2)}) copy-start(f32[8,1,256]{2,1,0:T(1,128)} %copy-done.60) | copy-start | bytes 24580
  1135.4 430.2 %copy-start.67 = (f32[256]{0:T(256)S(1)}, f32[256]{0:T(256)}, u32[]{:S(2)}) copy-start(f32[256]{0:T(256)} %copy-done.66) | copy-start | bytes 3076
  1135.4 430.2 %copy-start.69 = (f32[256]{0:T(256)S(1)}, f32[256]{0:T(256)}, u32[]{:S(2)}) copy-start(f32[256]{0:T(256)} %copy-done.68) | copy-start | bytes 3076
  1602.1 357.2 %copy-start.86 = (f32[256]{0:T(256)}, f32[256]{0:T(256)S(1)}, u32[]{:S(2)}) copy-start(f32[256]{0:T(256)S(1)} %dynamic-slice.4) | copy-start | bytes 3076
  (102 other events, 590.0 us)
Sparse Core Ops, SparseCore 0:
  9.9 30.9 all-gather.23
  42.5 80.7 all-gather.37
  124.8 79.2 all-gather.35
  206.2 79.2 all-gather.31
  287.2 44.0 all-gather.21
  332.7 80.7 all-gather.19
  415.1 79.2 all-gather.33
  496.3 52.9 all-gather.27
  551.4 80.7 all-gather.25
  633.9 54.4 all-gather.29
  706.9 144.4 reduce-scatter.10
  853.6 145.1 reduce-scatter.8
  1001.2 281.0 reduce-scatter.14
  1284.6 281.0 reduce-scatter.12
  1569.4 52.2 reduce-scatter.18
  1626.1 92.3 reduce-scatter.16
  1722.9 115.9 reduce-scatter.20
  1843.3 115.9 reduce-scatter.22
where the time goes:
time: 1980 us; the launch traced here: 1970 us
  waiting for transfers between devices  1190 us (60%)
  matrix products  399 us (20%)
  local copies, waits for them, and re-layouts  143 us (7%)
  blocking collectives  112 us (6%)
  other arithmetic  96.1 us (5%)
    reduce_scatter x2, waiting for transfers between devices, shards(): lax.psum_scatter(jnp.concatenate([times_transposed(grad_projected, qkv_ma...  426 us
    all_gather x2, waiting for transfers between devices, shards(): lax.all_gather(normed_one, 'tp', axis=0, tiled=True)  130 us
    reduce_scatter x1, waiting for transfers between devices, reduce_grads(): lax.psum_scatter(grad_set[4], 'fsdp', scatter_dimension=0, tiled=True)  120 us
    reduce_scatter x1, waiting for transfers between devices, reduce_grads(): lax.psum_scatter(grad_set[6], 'fsdp', scatter_dimension=1, tiled=True)  120 us
    all_gather x2, waiting for transfers between devices, shards(): lax.all_gather(out_grad[micro_step], 'tp', axis=0, tiled=True)  114 us
    dot_general x8, matrix products, inner_rows(): lax.dot_general(first_arr, second_arr, (((0,), (0,)), ((), ())), preferre...  99.6 us
    dot_general x8, matrix products, times_transposed(): lax.dot_general(first_arr, second_arr, (((1,), (1,)), ((), ())), preferre...  97.3 us
    reduce_scatter x1, waiting for transfers between devices, reduce_grads(): lax.psum_scatter(grad_set[0], 'fsdp', scatter_dimension=0, tiled=True)  93.4 us
  transfers between devices with their start and end apart: 18, of which 14 were waited for; matrix products, arithmetic and copies ran while one was open for 31% of the time, Pallas kernels for 0%

commit v1 on v0

v1 whole, which is shorter than its diff:
```python
from functools import partial
import math

import jax
import jax.numpy as jnp
from jax import lax
from jax.experimental import pallas as pl
from jax.experimental.pallas import tpu as pltpu
from jax.sharding import PartitionSpec as P

HEAD = 128
ROT = 32
EPSILON = 1e-05
MASKED = -1e30
F32 = jnp.float32
BF16 = jnp.bfloat16
VMEM_BYTES = 60 << 20


def dot_nn(a, b):
    return lax.dot_general(a, b, (((1,), (0,)), ((), ())), preferred_element_type=F32)


def dot_nt(a, b):
    return lax.dot_general(a, b, (((1,), (1,)), ((), ())), preferred_element_type=F32)


def dot_tn(a, b):
    return lax.dot_general(a, b, (((0,), (0,)), ((), ())), preferred_element_type=F32)


def row_stats(rows):
    mean = jnp.mean(rows, axis=-1, keepdims=True)
    centred = rows - mean
    spread = jnp.mean(centred * centred, axis=-1, keepdims=True)
    rstd = lax.rsqrt(spread + EPSILON)
    return centred * rstd, rstd


def rotary_full(row_count):
    half = ROT // 2
    exponent = jnp.arange(0, ROT, 2).astype(F32) / ROT
    inverse = 1.0 / 10000.0**exponent
    angles = jnp.arange(row_count).astype(F32)[:, None] * inverse[None, :]
    cosine, sine = jnp.cos(angles), jnp.sin(angles)
    rest = jnp.ones((row_count, HEAD - ROT), F32)
    return (
        jnp.concatenate([cosine, cosine, rest], axis=1),
        jnp.concatenate([-sine, sine, 0.0 * rest], axis=1),
    )


def swap_halves(block):
    half = ROT // 2
    lane = lax.broadcasted_iota(jnp.int32, block.shape, 1)
    return jnp.where(lane < half, pltpu.roll(block, HEAD - half, 1), pltpu.roll(block, half, 1))


def attention_kernel(
    row_tiles, heads, tile, len_ref, x_ref, c_ref, wqkv_ref, bqkv_ref, wo_ref, gain_ref, shift_ref,
    cos_ref, sin_ref, n1_ref, att_ref, gp_ref, q_s, k_s, v_s, ga_s, dk_s, dv_s,
):
    step = pl.program_id(0)
    length = len_ref[0]
    scale = 1.0 / math.sqrt(HEAD)

    @pl.when(step < row_tiles)
    def _():
        rows = pl.ds(pl.multiple_of(step * tile, tile), tile)
        xhat, _ = row_stats(x_ref[...].astype(F32))
        normed = (xhat * gain_ref[...] + shift_ref[...]).astype(BF16)
        n1_ref[...] = normed
        cosine, sine = cos_ref[rows, :], sin_ref[rows, :]
        for h in range(heads):
            part = dot_nn(normed, wqkv_ref[:, h * 384:(h + 1) * 384]) + bqkv_ref[:, h * 384:(h + 1) * 384]
            q, k = part[:, :HEAD], part[:, HEAD:2 * HEAD]
            q_s[h, rows, :] = (q * cosine + swap_halves(q) * sine).astype(BF16)
            k_s[h, rows, :] = (k * cosine + swap_halves(k) * sine).astype(BF16)
            v_s[h, rows, :] = part[:, 2 * HEAD:].astype(BF16)
        place = step * tile + lax.broadcasted_iota(jnp.int32, c_ref.shape, 0)
        cot = jnp.where(place < length, c_ref[...], jnp.zeros_like(c_ref))
        width = wo_ref.shape[2]
        grad = jnp.zeros((tile, heads * HEAD), F32)
        for j in range(wo_ref.shape[0]):
            grad = grad + dot_nt(cot[:, j * width:(j + 1) * width], wo_ref[j])
        for h in range(heads):
            ga_s[h, rows, :] = grad[:, h * HEAD:(h + 1) * HEAD].astype(BF16)

    @pl.when(step >= row_tiles)
    def _():
        h = step - row_tiles
        dk_s[...] = jnp.zeros_like(dk_s)
        dv_s[...] = jnp.zeros_like(dv_s)
        for i in range(row_tiles):
            rows = slice(i * tile, (i + 1) * tile)
            seen = slice(0, (i + 1) * tile)
            q, k, v, ga = q_s[h, rows, :], k_s[h, seen, :], v_s[h, seen, :], ga_s[h, rows, :]
            scores = dot_nt(q, k) * scale
            place = i * tile + lax.broadcasted_iota(jnp.int32, scores.shape, 0)
            key = lax.broadcasted_iota(jnp.int32, scores.shape, 1)
            scores = jnp.where(key <= jnp.minimum(place, length - 1), scores, MASKED)
            top = jnp.max(scores, axis=-1, keepdims=True)
            raised = jnp.exp(scores - top)
            soft = raised * (1.0 / jnp.sum(raised, axis=-1, keepdims=True))
            probs = soft.astype(BF16)
            att_ref[rows, :] = dot_nn(probs, v).astype(BF16)
            grad_probs = dot_nt(ga, v)
            row_dot = jnp.sum(soft * grad_probs, axis=-1, keepdims=True)
            grad_scores = (soft * (grad_probs - row_dot)).astype(BF16)
            dq = dot_nn(grad_scores, k) * scale
            cosine, sine = cos_ref[rows, :], sin_ref[rows, :]
            gp_ref[rows, 0:HEAD] = (dq * cosine - swap_halves(dq) * sine).astype(BF16)
            dk_s[seen, :] += dot_tn(grad_scores, q)
            dv_s[seen, :] += dot_tn(probs, ga)
        dk = dk_s[...] * scale
        gp_ref[:, HEAD:2 * HEAD] = (dk * cos_ref[...] - swap_halves(dk) * sin_ref[...]).astype(BF16)
        gp_ref[:, 2 * HEAD:] = dv_s[...].astype(BF16)


def whole(shape):
    return pl.BlockSpec(shape, lambda i: (0,) * len(shape), pipeline_mode=pl.Buffered(1))


def attention_call(length, x, c, wqkv, bqkv, wo, gain, shift, cos, sin):
    slot, width = x.shape
    heads = wqkv.shape[1] // (3 * HEAD)
    tile = 256
    row_tiles = slot // tile
    row_block = pl.BlockSpec((tile, width), lambda i: (jnp.minimum(i, row_tiles - 1), 0))
    head_at = lambda i: (0, jnp.maximum(i - row_tiles, 0))
    return pl.pallas_call(
        partial(attention_kernel, row_tiles, heads, tile),
        grid=(row_tiles + heads,),
        in_specs=[
            pl.BlockSpec(memory_space=pltpu.SMEM), row_block, row_block, whole(wqkv.shape), whole(bqkv.shape),
            whole(wo.shape), whole(gain.shape), whole(shift.shape), whole(cos.shape), whole(sin.shape),
        ],
        out_specs=[row_block, pl.BlockSpec((slot, HEAD), head_at), pl.BlockSpec((slot, 3 * HEAD), head_at)],
        out_shape=[
            jax.ShapeDtypeStruct((slot, width), BF16),
            jax.ShapeDtypeStruct((slot, heads * HEAD), BF16),
            jax.ShapeDtypeStruct((slot, heads * 3 * HEAD), BF16),
        ],
        scratch_shapes=[pltpu.VMEM((heads, slot, HEAD), BF16)] * 4 + [pltpu.VMEM((slot, HEAD), F32)] * 2,
        compiler_params=pltpu.CompilerParams(
            dimension_semantics=("arbitrary",), vmem_limit_bytes=VMEM_BYTES
        ),
        cost_estimate=pl.CostEstimate(flops=int(14e9), bytes_accessed=int(20e6), transcendentals=int(3e6)),
    )(length, x, c, wqkv, bqkv, wo, gain, shift, cos, sin)


def normal_pair(value):
    density = jnp.exp(-0.5 * value * value)
    t = 1.0 / (1.0 + (0.3275911 * math.sqrt(0.5)) * jnp.abs(value))
    series = ((((1.061405429 * t - 1.453152027) * t) + 1.421413741) * t - 0.284496736) * t + 0.254829592
    tail = (0.5 * t) * series * density
    return jnp.where(value >= 0, 1.0 - tail, tail), density * (1.0 / math.sqrt(2.0 * math.pi))


def feed_kernel(
    tile, chunk, len_ref, x_ref, c_ref, att_ref, gp_ref, w1_ref, w2_ref, wo_ref, wqkv_ref, b1_ref,
    gain1_ref, gain2_ref, shift2_ref, n2_ref, act_ref, gpre_ref, h_ref, u_ref, sd_ref, sf_ref, sq_ref, xhat_s, cot_s,
):
    step = pl.program_id(0)
    length = len_ref[0]
    blocks, hidden, width = w2_ref.shape
    model = x_ref.shape[1]

    @pl.when(step == 0)
    def _():
        sd_ref[...] = jnp.zeros_like(sd_ref)
        sf_ref[...] = jnp.zeros_like(sf_ref)
        sq_ref[...] = jnp.zeros_like(sq_ref)

    xhat, _ = row_stats(x_ref[...].astype(F32))
    xhat_s[...] = xhat
    n2_ref[...] = (xhat * gain2_ref[...] + shift2_ref[...]).astype(BF16)
    place = step * tile + lax.broadcasted_iota(jnp.int32, c_ref.shape, 0)
    cot_s[...] = jnp.where(place < length, c_ref[...], jnp.zeros_like(c_ref))
    ones = jnp.ones((8, tile), BF16)
    for k in range(hidden // chunk):
        cols = slice(k * chunk, (k + 1) * chunk)
        pre = dot_nn(n2_ref[...], w1_ref[:, cols]) + b1_ref[:, cols]
        below, density = normal_pair(pre)
        act_ref[:, cols] = (pre * below).astype(BF16)
        gact = dot_nt(cot_s[:, 0:width], w2_ref[0, cols, :])
        for j in range(1, blocks):
            gact = gact + dot_nt(cot_s[:, j * width:(j + 1) * width], w2_ref[j, cols, :])
        gpre = (gact * (below + pre * density)).astype(BF16)
        gpre_ref[:, cols] = gpre
        sf_ref[:, cols] += dot_nn(ones, gpre)
    sq_ref[...] += dot_nn(ones, gp_ref[...])
    for j in range(blocks):
        cols = slice(j * width, (j + 1) * width)
        h_ref[:, cols] = (dot_nn(act_ref[...], w2_ref[j]) + dot_nn(att_ref[...], wo_ref[j])).astype(BF16)
    for k in range(model // chunk):
        cols = slice(k * chunk, (k + 1) * chunk)
        g2 = dot_nt(gpre_ref[...], w1_ref[cols, :])
        g1 = dot_nt(gp_ref[...], wqkv_ref[cols, :])
        u_ref[:, cols] = (g1 * gain1_ref[:, cols] + g2 * gain2_ref[:, cols]).astype(BF16)
        hat = xhat_s[:, cols]
        sd_ref[0:1, cols] += jnp.sum(g1 * hat, axis=0, keepdims=True)
        sd_ref[1:2, cols] += jnp.sum(g1, axis=0, keepdims=True)
        sd_ref[2:3, cols] += jnp.sum(g2 * hat, axis=0, keepdims=True)
        sd_ref[3:4, cols] += jnp.sum(g2, axis=0, keepdims=True)
        sd_ref[4:5, cols] += dot_nn(ones, cot_s[:, cols])[0:1]


def feed_call(length, x, c, att, gp, w1, w2, wo, wqkv, b1, gain1, gain2, shift2):
    slot, width = x.shape
    hidden = w1.shape[1]
    tile, chunk = 256, 512
    at = lambda i: (i, 0)
    keep = lambda i: (0, 0)
    row_block = pl.BlockSpec((tile, width), at)
    hid_block = pl.BlockSpec((tile, hidden), at)
    return pl.pallas_call(
        partial(feed_kernel, tile, chunk),
        grid=(slot // tile,),
        in_specs=[
            pl.BlockSpec(memory_space=pltpu.SMEM), row_block, row_block, pl.BlockSpec((tile, att.shape[1]), at),
            pl.BlockSpec((tile, gp.shape[1]), at), whole(w1.shape), whole(w2.shape), whole(wo.shape),
            whole(wqkv.shape), whole(b1.shape), whole(gain1.shape), whole(gain2.shape), whole(shift2.shape),
        ],
        out_specs=[
            row_block, hid_block, hid_block, row_block, row_block,
            pl.BlockSpec((8, width), keep), pl.BlockSpec((8, hidden), keep), pl.BlockSpec((8, gp.shape[1]), keep),
        ],
        out_shape=[
            jax.ShapeDtypeStruct((slot, width), BF16),
            jax.ShapeDtypeStruct((slot, hidden), BF16),
            jax.ShapeDtypeStruct((slot, hidden), BF16),
            jax.ShapeDtypeStruct((slot, width), BF16),
            jax.ShapeDtypeStruct((slot, width), BF16),
            jax.ShapeDtypeStruct((8, width), F32),
            jax.ShapeDtypeStruct((8, hidden), F32),
            jax.ShapeDtypeStruct((8, gp.shape[1]), F32),
        ],
        scratch_shapes=[pltpu.VMEM((tile, width), F32), pltpu.VMEM((tile, width), BF16)],
        compiler_params=pltpu.CompilerParams(
            dimension_semantics=("arbitrary",), vmem_limit_bytes=VMEM_BYTES
        ),
        cost_estimate=pl.CostEstimate(flops=int(45e9), bytes_accessed=int(50e6), transcendentals=int(4e6)),
    )(length, x, c, att, gp, w1, w2, wo, wqkv, b1, gain1, gain2, shift2)


def shards(
    hidden_in, out_grad, lengths, qkv_weight, qkv_bias, out_weight, out_bias, fc1_weight, fc1_bias,
    fc2_weight, fc2_bias, ln1_gain, ln1_bias, ln2_gain, ln2_bias,
):
    tp_size = lax.axis_size("tp")
    tp_index = lax.axis_index("tp")
    fsdp_index = lax.axis_index("fsdp")
    micro_count, shard_rows, model = hidden_in.shape
    slot = shard_rows * tp_size
    own = out_bias.shape[0]
    cos, sin = rotary_full(slot)
    gather = lambda value, axis: lax.all_gather(value, axis, axis=0, tiled=True)

    small = (qkv_bias, fc1_bias, out_bias, fc2_bias, ln1_gain, ln1_bias, ln2_gain, ln2_bias)
    packed = lax.all_gather(jnp.concatenate(small), "fsdp", axis=0, tiled=False).astype(F32)
    rows, start = [], 0
    for value in small:
        rows.append(packed[:, start:start + value.shape[0]].reshape(1, -1))
        start += value.shape[0]
    bqkv, b1, bo, b2, gain1, shift1, gain2, shift2 = rows
    wqkv = gather(qkv_weight, "fsdp")
    wo = lax.all_gather(out_weight, "fsdp", axis=0, tiled=False)
    w1 = gather(fc1_weight, "fsdp")
    w2 = lax.all_gather(fc2_weight, "fsdp", axis=0, tiled=False)

    parts, outputs, in_grads = [], [], []
    for m in range(micro_count):
        length = lengths[m]
        x = gather(hidden_in[m], "tp")
        c = gather(out_grad[m], "tp")
        n1, att, gp = attention_call(length, x, c, wqkv, bqkv, wo, gain1, shift1, cos, sin)
        n2, act, gpre, h, u, sd, sf, sq = feed_call(
            length, x, c, att, gp, w1, w2, wo, wqkv, b1, gain1, gain2, shift2
        )
        valid = (jnp.arange(slot) < length[0])[:, None]
        cot = jnp.where(valid, c, jnp.zeros_like(c))
        parts.append((n1, att, gp, n2, act, gpre, cot, sd, sf, sq))
        h_own = lax.psum_scatter(h, "tp", scatter_dimension=0, tiled=True)
        u_own = lax.psum_scatter(u, "tp", scatter_dimension=0, tiled=True).astype(F32)
        live = (tp_index * shard_rows + jnp.arange(shard_rows) < length[0])[:, None]
        local = hidden_in[m].astype(F32)
        result = local + h_own.astype(F32) + bo + b2
        outputs.append(jnp.where(live, result, 0.0).astype(BF16))
        xhat, rstd = row_stats(local)
        back = rstd * (
            u_own - jnp.mean(u_own, axis=-1, keepdims=True)
            - xhat * jnp.mean(u_own * xhat, axis=-1, keepdims=True)
        )
        in_grads.append((jnp.where(live, out_grad[m].astype(F32), 0.0) + back).astype(BF16))

    def weight_grad(left, right):
        total = dot_tn(parts[0][left], parts[0][right])
        for part in parts[1:]:
            total = total + dot_tn(part[left], part[right])
        return lax.psum_scatter(total.astype(BF16), "fsdp", scatter_dimension=0, tiled=True).astype(F32)

    grad_up = weight_grad(3, 5)
    grad_down = weight_grad(6, 4).T
    grad_qkv = weight_grad(0, 2)
    grad_out = weight_grad(6, 1).T
    sums = [sum(part[7 + k] for part in parts) for k in range(3)]
    flat = lax.psum(
        jnp.concatenate([sums[0][:5].reshape(-1), sums[1][0], sums[2][0]]), "fsdp"
    )
    wide = 5 * model
    norm = lax.dynamic_slice_in_dim(flat[:wide].reshape(5, model), fsdp_index * own, own, 1)
    ln = lax.psum(norm[:4], "tp")
    own_f, own_q = fc1_bias.shape[0], qkv_bias.shape[0]
    grad_b1 = lax.dynamic_slice_in_dim(flat[wide:wide + w1.shape[1]], fsdp_index * own_f, own_f, 0)
    grad_bq = lax.dynamic_slice_in_dim(flat[wide + w1.shape[1]:], fsdp_index * own_q, own_q, 0)
    return (
        jnp.stack(outputs), jnp.stack(in_grads), grad_qkv, grad_bq, grad_out, norm[4], grad_up, grad_b1,
        grad_down, norm[4], ln[0], ln[1], ln[2], ln[3],
    )


def solution(mesh):
    rows = P(None, ("fsdp", "tp"), None)
    both, column, row, one = P(("tp", "fsdp")), P("fsdp", "tp"), P("tp", "fsdp"), P("fsdp")
    return jax.shard_map(
        shards,
        mesh=mesh,
        in_specs=(rows, rows, P(None, "fsdp"), column, both, row, one, column, both, row, one, one, one, one, one),
        out_specs=(rows, rows, column, both, row, one, column, both, row, one, one, one, one, one),
        check_vma=False,
    )
```

time: 1980 us -> 1120 us (0.57)
  waiting for transfers between devices: 1190 us -> 680 us
  matrix products: 399 us -> 96.4 us
  Pallas kernels: 0 us -> 217 us
  local copies, waits for them, and re-layouts: 143 us -> 17 us
  other arithmetic: 96.1 us -> 27.1 us
  blocking collectives: 112 us -> 61.9 us
    reduce_scatter x8, waiting for transfers between devices: 760 us -> 315 us  [the longest x4 138 us: weight_grad(): lax.psum_scatter(total.astype(BF16), 'fsdp', scatter_dimension=0, tiled=T...]
    dot_general x52 -> x8, matrix products: 399 us -> 96.4 us  [dot_tn(): lax.dot_general(a, b, (((0,), (0,)), ((), ())), preferred_element_type=F32)]
    pallas_call x0 -> x4, Pallas kernels: none -> 217 us  [the longest x2 138 us: feed_call(): pl.pallas_call(partial(feed_kernel, tile, chunk), grid=(slot // tile,), i...]
    all_gather x10 -> x8, waiting for transfers between devices: 425 us -> 360 us  [the longest x6 317 us: shards(): gather = lambda value, axis: lax.all_gather(value, axis, axis=0, tiled=True)]
    all_gather x7 -> x0, blocking collectives: 61.1 us -> none  [the longest x1 10.3 us: fetch_weights(): lax.all_gather(ln2_bias, 'fsdp', axis=0, tiled=True)]
    dynamic_update_slice x8 -> x0, local copies, waits for them, and re-layouts: 48.3 us -> none  [the longest x4 46.6 us: shards(): lax.scan(back_block, (zero_rows, zero_rows), (jnp.arange(block_count), lo...]
    reduce_sum x12 -> x4, other arithmetic: 31 us -> 6.69 us  [the longest x1 3.61 us: shards(): jnp.mean(u_own, axis=-1, keepdims=True)]
    psum x1 -> x2, blocking collectives: 12.2 us -> 36.1 us  [the longest x1 23.8 us: shards(): lax.psum(jnp.concatenate([sums[0][:5].reshape(-1), sums[1][0], sums[2][0]...]
  transfers between devices with their start and end apart: 18 -> 16, of which waited for: 14 -> 11; matrix products, arithmetic and copies ran while one was open for 31% -> 12% of each run, Pallas kernels for 0% -> 19%
where the time goes in v1:
time: 1120 us
  waiting for transfers between devices  680 us (61%)
  Pallas kernels  217 us (19%)
  matrix products  96.4 us (9%)
  blocking collectives  61.9 us (6%)
  other arithmetic  27.1 us (2%)
  local copies, waits for them, and re-layouts  17 us (2%)
  between operations  15.4 us (1%)
    all_gather x6, waiting for transfers between devices, shards(): gather = lambda value, axis: lax.all_gather(value, axis, axis=0, tiled=True)  317 us
    pallas_call x2, Pallas kernels, feed_call(): pl.pallas_call(partial(feed_kernel, tile, chunk), grid=(slot // tile,), i...  138 us
    reduce_scatter x4, waiting for transfers between devices, weight_grad(): lax.psum_scatter(total.astype(BF16), 'fsdp', scatter_dimension=0, tiled=T...  138 us
    reduce_scatter x2, waiting for transfers between devices, shards(): h_own = lax.psum_scatter(h, 'tp', scatter_dimension=0, tiled=True)  97.1 us
    dot_general x8, matrix products, dot_tn(): lax.dot_general(a, b, (((0,), (0,)), ((), ())), preferred_element_type=F32)  96.4 us
    reduce_scatter x2, waiting for transfers between devices, shards(): lax.psum_scatter(u, 'tp', scatter_dimension=0, tiled=True).astype(F32)  79.6 us
    pallas_call x2, Pallas kernels, attention_call(): pl.pallas_call(partial(attention_kernel, row_tiles, heads, tile), grid=(r...  78.9 us
    all_gather x1, waiting for transfers between devices, shards(): w2 = lax.all_gather(fc2_weight, 'fsdp', axis=0, tiled=False)  42.6 us
  transfers between devices with their start and end apart: 16, of which 11 were waited for; matrix products, arithmetic and copies ran while one was open for 12% of the time, Pallas kernels for 19%

profile of v1, /device:TPU:0, one launch (start us, length us, event | category | flops | bytes accessed | tf_op | source)
XLA Modules:
  0.0 1115.1 jit_solution(10833272122760626470)
XLA Ops:
  8.0 3.2 fusion.48
  18.0 25.8 %all-reduce = bf16[15872]{0:T(1024)(128)(2,1)S(1)} all-reduce(bf16[15872]{0:T(1024)(128)(2,1)S(1)} %dynamic-update-slice), channel_id=4, replica_groups=mesh['fsdp'=8,'tp'=4] {'fsdp'}, use_global_device_ids=true, to_apply=%add | all-reduce | flops 15872 | bytes 63488
  51.6 72.2 %all-gather.22.cloned.1.call-done = bf16[1,1024,2048]{2,1,0:T(8,128)(2,1)} async-done(((bf16[1,256,2048]{2,1,0:T(8,128)(2,1)}), bf16[1,1024,2048]{2,1,0:T(8,128)(2,1)}) %all-gather.22.cloned.1.call-update) | async-done | bytes 4194320 | tf_op jit(solution)/shard_map/all_gather | solution.py:258
  123.7 81.5 %all-gather.20.cloned.1.call-done = bf16[1,1024,2048]{2,1,0:T(8,128)(2,1)} async-done(((bf16[1,256,2048]{2,1,0:T(8,128)(2,1)}), bf16[1,1024,2048]{2,1,0:T(8,128)(2,1)}) %all-gather.20.cloned.1.call-update) | async-done | bytes 4194320 | tf_op jit(solution)/shard_map/all_gather | solution.py:258
  205.2 45.8 %all-gather.16.cloned.1.call-done.wqkv_ref = bf16[2048,1536]{1,0:T(8,128)(2,1)} async-done(((bf16[256,1536]{1,0:T(8,128)(2,1)}), bf16[2048,1536]{1,0:T(8,128)(2,1)}) %all-gather.16.cloned.1.call-update) | async-done | bytes 6291472 | tf_op jit(solution)/shard_map/all_gather | solution.py:258
  251.0 39.3 %shard_map.254 = (bf16[1024,2048]{1,0:T(8,128)(2,1)}, bf16[1024,512]{1,0:T(8,128)(2,1)}, bf16[1024,1536]{1,0:T(8,128)(2,1)}) custom-call(s32[1]{0:T(128)} %bitcast.2.len_ref, bf16[1024,2048]{1,0:T(8,128)(2,1)} %bitcast.192, bf16[1024,2048]{1,0:T(8,128)(2,1)} %bitcast.188, bf16[2048,1536]{1,0:T(8,128)(2,1)} %all-gather.16.cloned.1.call-done.wqkv_ref, ...), custom_call_target="tpu_custom_call" | custom-call | flops 14000000000 | bytes 20000000 | tf_op jit(solution)/shard_map/pallas_call | solution.py:131
  290.3 7.0 fusion.31
  297.3 36.5 %all-gather.30.cloned.1.call-done = bf16[1,1024,2048]{2,1,0:T(8,128)(2,1)} async-done(((bf16[1,256,2048]{2,1,0:T(8,128)(2,1)}), bf16[1,1024,2048]{2,1,0:T(8,128)(2,1)}) %all-gather.30.cloned.1.call-update) | async-done | bytes 4194320 | tf_op jit(solution)/shard_map/all_gather | solution.py:258
  333.8 81.3 %all-gather.28.cloned.1.call-done = bf16[1,1024,2048]{2,1,0:T(8,128)(2,1)} async-done(((bf16[1,256,2048]{2,1,0:T(8,128)(2,1)}), bf16[1,1024,2048]{2,1,0:T(8,128)(2,1)}) %all-gather.28.cloned.1.call-update) | async-done | bytes 4194320 | tf_op jit(solution)/shard_map/all_gather | solution.py:258
  415.1 39.6 %shard_map.256 = (bf16[1024,2048]{1,0:T(8,128)(2,1)}, bf16[1024,512]{1,0:T(8,128)(2,1)}, bf16[1024,1536]{1,0:T(8,128)(2,1)}) custom-call(s32[1]{0:T(128)} %bitcast.11.len_ref, bf16[1024,2048]{1,0:T(8,128)(2,1)} %bitcast.194, bf16[1024,2048]{1,0:T(8,128)(2,1)} %bitcast.190, bf16[2048,1536]{1,0:T(8,128)(2,1)} %all-gather.16.cloned.1.call-done.wqkv_ref, ...), custom_call_target="tpu_custom_call" | custom-call | flops 14000000000 | bytes 20000000 | tf_op jit(solution)/shard_map/pallas_call | solution.py:131
  454.7 7.8 add_convert_fusion.3
  462.6 10.0 fusion.52
  472.6 9.2 add_convert_fusion.2
  483.7 42.6 %all-gather.26.cloned.1.call-done = bf16[16384,256]{1,0:T(8,128)(2,1)} async-done(((bf16[2048,256]{1,0:T(8,128)(2,1)}), bf16[16384,256]{1,0:T(8,128)(2,1)}) %all-gather.26.cloned.1.call-update) | async-done | bytes 8388624 | tf_op jit(solution)/shard_map/all_gather | solution.py:270
  526.3 68.5 %shard_map.255 = (bf16[1024,2048]{1,0:T(8,128)(2,1)}, bf16[1024,2048]{1,0:T(8,128)(2,1)}, bf16[1024,2048]{1,0:T(8,128)(2,1)}, bf16[1024,2048]{1,0:T(8,128)(2,1)}...) custom-call(s32[1]{0:T(128)} %bitcast.2.len_ref, ...), custom_call_target="tpu_custom_call" | custom-call | flops 44999999488 | bytes 50000000 | tf_op jit(solution)/shard_map/pallas_call | solution.py:217
  594.8 69.7 %shard_map.257 = (bf16[1024,2048]{1,0:T(8,128)(2,1)}, bf16[1024,2048]{1,0:T(8,128)(2,1)}, bf16[1024,2048]{1,0:T(8,128)(2,1)}, bf16[1024,2048]{1,0:T(8,128)(2,1)}...) custom-call(s32[1]{0:T(128)} %bitcast.11.len_ref, ...), custom_call_target="tpu_custom_call" | custom-call | flops 44999999488 | bytes 50000000 | tf_op jit(solution)/shard_map/pallas_call | solution.py:217
  666.0 15.6 %fusion.30 = f32[2048,2048]{1,0:T(8,128)} fusion(bf16[1024,2048]{1,0:T(8,128)(2,1)} %get-tuple-element.56, pred[1024]{0:T(1024)(128)(4,1)S(1)} %iota_compare_fusion.1, bf16[1,1024,2048]{2,1,0:T(8,128)(2,1)} %all-gather.22.cloned.1.call-done), kind=kOutput, calls=%fused_computation.51 | convolution fusion | flops 8592031744 | bytes 25166848 | tf_op jit(solution)/shard_map/dot_general | solution.py:29
  681.6 16.1 %add_convert_fusion = bf16[2048,2048]{1,0:T(8,128)(2,1)} fusion(f32[2048,2048]{1,0:T(8,128)} %fusion.30, bf16[1024,2048]{1,0:T(8,128)(2,1)} %get-tuple-element.57, pred[1024]{0:T(1024)(128)(4,1)S(1)} %iota_compare_fusion, bf16[1,1024,2048]{2,1,0:T(8,128)(2,1)S(1)} %copy-done.19), kind=kOutput, calls=%fused_computation | convolution fusion | flops 8600420352 | bytes 33555456 | tf_op jit(solution)/shard_map/dot_general | solution.py:29
  697.8 15.9 %fusion.53 = f32[2048,2048]{1,0:T(8,128)} fusion(bf16[1024,2048]{1,0:T(8,128)(2,1)} %get-tuple-element.52, bf16[1024,2048]{1,0:T(8,128)(2,1)} %get-tuple-element.53), kind=kOutput, calls=%fused_computation.104 | convolution fusion | flops 8589934592 | bytes 25165824 | tf_op jit(solution)/shard_map/dot_general | solution.py:29
  713.7 14.8 %add_convert_fusion.1 = bf16[2048,2048]{1,0:T(8,128)(2,1)} fusion(f32[2048,2048]{1,0:T(8,128)} %fusion.53, bf16[1024,2048]{1,0:T(8,128)(2,1)S(1)} %copy-done.23, bf16[1024,2048]{1,0:T(8,128)(2,1)S(1)} %copy-done.24), kind=kOutput, calls=%fused_computation.1 | convolution fusion | flops 8598323200 | bytes 33554432 | tf_op jit(solution)/shard_map/dot_general | solution.py:29
  735.2 23.8 %psum.14 = f32[13824]{0:T(1024)S(1)} all-reduce(f32[13824]{0:T(1024)S(1)} %pad_maximum_fusion.2), channel_id=1, replica_groups=mesh['fsdp'=8,'tp'=4] {'fsdp'}, use_global_device_ids=true, to_apply=%region_13.14 | all-reduce | flops 13824 | bytes 110592 | tf_op jit(solution)/shard_map/psum | solution.py:308
  760.4 12.3 %psum.15 = f32[4,256]{1,0:T(4,128)S(1)} all-reduce(f32[4,256]{1,0:T(4,128)S(1)} %constant_dynamic-slice_fusion), channel_id=1, replica_groups=mesh['fsdp'=8,'tp'=4] {'tp'}, use_global_device_ids=true, to_apply=%region_17.18 | all-reduce | flops 1024 | bytes 8192 | tf_op jit(solution)/shard_map/psum | solution.py:313
  773.3 2.5 convert_element_type.101
  775.8 2.3 fusion.28
  778.1 17.6 %reduce-scatter.11.cloned.1.call-done = bf16[256,2048]{1,0:T(8,128)(2,1)} async-done(((bf16[1024,2048]{1,0:T(8,128)(2,1)}), bf16[256,2048]{1,0:T(8,128)(2,1)}) %reduce-scatter.11.cloned.1.call-update) | async-done | bytes 1048592 | tf_op jit(solution)/shard_map/reduce_scatter | solution.py:284
  795.7 79.6 %reduce-scatter.15.cloned.1.call-done = bf16[256,2048]{1,0:T(8,128)(2,1)} async-done(((bf16[1024,2048]{1,0:T(8,128)(2,1)}), bf16[256,2048]{1,0:T(8,128)(2,1)}) %reduce-scatter.15.cloned.1.call-update) | async-done | bytes 1048592 | tf_op jit(solution)/shard_map/reduce_scatter | solution.py:285
  875.3 79.5 %reduce-scatter.9.cloned.1.call-done = bf16[256,2048]{1,0:T(8,128)(2,1)} async-done(((bf16[1024,2048]{1,0:T(8,128)(2,1)}), bf16[256,2048]{1,0:T(8,128)(2,1)}) %reduce-scatter.9.cloned.1.call-update) | async-done | bytes 1048592 | tf_op jit(solution)/shard_map/reduce_scatter | solution.py:284
  954.9 3.6 convert_reduce_fusion
  958.5 2.1 fusion.35
  963.6 66.3 %reduce-scatter.23.cloned.1.call-done = bf16[256,2048]{1,0:T(8,128)(2,1)} async-done(((bf16[2048,2048]{1,0:T(8,128)(2,1)}), bf16[256,2048]{1,0:T(8,128)(2,1)}) %reduce-scatter.23.cloned.1.call-update) | async-done | bytes 1048592 | tf_op jit(solution)/shard_map/reduce_scatter | solution.py:301
  1033.2 71.7 %reduce-scatter.21.cloned.1.call-done = bf16[256,2048]{1,0:T(8,128)(2,1)} async-done(((bf16[2048,2048]{1,0:T(8,128)(2,1)}), bf16[256,2048]{1,0:T(8,128)(2,1)}) %reduce-scatter.21.cloned.1.call-update) | async-done | bytes 1048592 | tf_op jit(solution)/shard_map/reduce_scatter | solution.py:301
  1105.0 2.8 convert_element_type.104
  (146 shorter events, 33.2 us)
Async XLA Ops:
  7.2 44.4 %all-gather.24.cloned.1.call-start = ((), (), s32[]{:S(2)}) async-start(), calls=%async_computation.20 | async-start | bytes 2359296 | tf_op jit(solution)/shard_map/all_gather | solution.py:268
  7.9 115.8 %all-gather.22.cloned.1.call-start = ((), (), s32[]{:S(2)}) async-start(), calls=%async_computation.19 | async-start | bytes 5242880 | tf_op jit(solution)/shard_map/all_gather | solution.py:258
  11.2 193.9 %all-gather.20.cloned.1.call-start = ((), (), s32[]{:S(2)}) async-start(), calls=%async_computation.18 | async-start | bytes 5242880 | tf_op jit(solution)/shard_map/all_gather | solution.py:258
  12.8 238.2 %all-gather.16.cloned.1.call-start = ((), (), s32[]{:S(2)}) async-start(), calls=%async_computation.8 | async-start | bytes 7077888 | tf_op jit(solution)/shard_map/all_gather | solution.py:258
  13.4 320.4 %all-gather.30.cloned.1.call-start = ((), (), s32[]{:S(2)}) async-start(), calls=%async_computation.23 | async-start | bytes 5242880 | tf_op jit(solution)/shard_map/all_gather | solution.py:258
  13.4 4.1 copy-start.11
  13.4 4.1 copy-start.12
  13.4 4.1 copy-start.13
  13.4 4.1 copy-start.14
  13.5 4.1 copy-start.15
  13.5 4.1 copy-start.16
  13.5 4.1 copy-start.17
  13.5 4.0 copy-start.18
  13.5 32.9 %copy-start.10 = (s32[2,1]{0,1:T(1,128)S(1)}, s32[2,1]{0,1:T(1,128)}, u32[]{:S(2)}) copy-start(s32[2,1]{0,1:T(1,128)} %param.17) | copy-start | bytes 28
  13.9 401.2 %all-gather.28.cloned.1.call-start = ((), (), s32[]{:S(2)}) async-start(), calls=%async_computation.22 | async-start | bytes 5242880 | tf_op jit(solution)/shard_map/all_gather | solution.py:258
  14.5 469.2 %all-gather.18.cloned.1.call-start = ((), (), s32[]{:S(2)}) async-start(), calls=%async_computation.9 | async-start | bytes 9437184 | tf_op jit(solution)/shard_map/all_gather | solution.py:258
  15.3 511.0 %all-gather.26.cloned.1.call-start = ((), (), s32[]{:S(2)}) async-start(), calls=%async_computation.21 | async-start | bytes 9437184 | tf_op jit(solution)/shard_map/all_gather | solution.py:270
  16.0 715.3 %reduce-scatter.19.cloned.1.call-start = ((), (), s32[]{:S(2)}) async-start(), calls=%async_computation.15 | async-start | bytes 2359296 | tf_op jit(solution)/shard_map/reduce_scatter | solution.py:301
  462.5 310.8 %reduce-scatter.17.cloned.1.call-start = ((), (), s32[]{:S(2)}) async-start(), calls=%async_computation.14 | async-start | bytes 7077888 | tf_op jit(solution)/shard_map/reduce_scatter | solution.py:301
  462.6 10.1 copy-start.21
  462.6 10.1 copy-start.22
  481.8 293.9 %reduce-scatter.13.cloned.1.call-start = ((), (), s32[]{:S(2)}) async-start(), calls=%async_computation.12 | async-start | bytes 5242880 | tf_op jit(solution)/shard_map/reduce_scatter | solution.py:285
  594.8 200.9 %reduce-scatter.11.cloned.1.call-start = ((), (), s32[]{:S(2)}) async-start(), calls=%async_computation.11 | async-start | bytes 5242880 | tf_op jit(solution)/shard_map/reduce_scatter | solution.py:284
  664.6 210.7 %reduce-scatter.15.cloned.1.call-start = ((), (), s32[]{:S(2)}) async-start(), calls=%async_computation.13 | async-start | bytes 5242880 | tf_op jit(solution)/shard_map/reduce_scatter | solution.py:285
  665.3 289.5 %reduce-scatter.9.cloned.1.call-start = ((), (), s32[]{:S(2)}) async-start(), calls=%async_computation.10 | async-start | bytes 5242880 | tf_op jit(solution)/shard_map/reduce_scatter | solution.py:284
  665.9 364.1 %reduce-scatter.23.cloned.1.call-start = ((), (), s32[]{:S(2)}) async-start(), calls=%async_computation.17 | async-start | bytes 9437184 | tf_op jit(solution)/shard_map/reduce_scatter | solution.py:301
  666.0 15.6 %copy-start.19 = (bf16[1,1024,2048]{2,1,0:T(8,128)(2,1)S(1)}, bf16[1,1024,2048]{2,1,0:T(8,128)(2,1)}, u32[]{:S(2)}) copy-start(bf16[1,1024,2048]{2,1,0:T(8,128)(2,1)} %all-gather.30.cloned.1.call-done) | copy-start | bytes 12582916
  697.7 407.3 %reduce-scatter.21.cloned.1.call-start = ((), (), s32[]{:S(2)}) async-start(), calls=%async_computation.16 | async-start | bytes 9437184 | tf_op jit(solution)/shard_map/reduce_scatter | solution.py:301
  697.8 15.9 %copy-start.23 = (bf16[1024,2048]{1,0:T(8,128)(2,1)S(1)}, bf16[1024,2048]{1,0:T(8,128)(2,1)}, u32[]{:S(2)}) copy-start(bf16[1024,2048]{1,0:T(8,128)(2,1)} %get-tuple-element.54) | copy-start | bytes 12582916
  697.8 15.9 %copy-start.24 = (bf16[1024,2048]{1,0:T(8,128)(2,1)S(1)}, bf16[1024,2048]{1,0:T(8,128)(2,1)}, u32[]{:S(2)}) copy-start(bf16[1024,2048]{1,0:T(8,128)(2,1)} %get-tuple-element.55) | copy-start | bytes 12582916
  759.8 348.0 %copy-start.9 = (f32[1,256]{1,0:T(1,128)}, f32[1,256]{1,0:T(1,128)S(1)}, u32[]{:S(2)}) copy-start(f32[1,256]{1,0:T(1,128)S(1)} %dynamic-slice.1) | copy-start | bytes 3076
  954.8 3.7 copy-start.4
  (9 other events, 22.7 us)
Sparse Core Ops, SparseCore 0:
  9.9 30.8 all-gather.23
  42.9 80.7 all-gather.21
  125.9 79.2 all-gather.19
  206.9 44.0 all-gather.15
  253.0 80.7 all-gather.29
  335.8 79.2 all-gather.27
  417.0 52.9 all-gather.17
  471.9 54.3 all-gather.25
  530.1 41.2 reduce-scatter.18
  575.0 61.7 reduce-scatter.16
  639.1 76.7 reduce-scatter.12
  718.1 77.5 reduce-scatter.10
  798.0 77.2 reduce-scatter.14
  877.5 77.2 reduce-scatter.8
  958.2 71.7 reduce-scatter.22
  1033.7 71.2 reduce-scatter.20

commit v2 on v1

--- a/solution.py
+++ b/solution.py
@@ -55,8 +55,201 @@
     lane = lax.broadcasted_iota(jnp.int32, block.shape, 1)
     return jnp.where(lane < half, pltpu.roll(block, HEAD - half, 1), pltpu.roll(block, half, 1))
 
-
-def attention_kernel(
+MESH = pl.DeviceIdType.MESH
+
+
+def greet(axes, lines):
+    barrier = pltpu.get_barrier_semaphore()
+    count = 0
+    for axis, size in axes:
+        here = lax.axis_index(axis)
+        for k in range(1, size):
+            pl.semaphore_signal(
+                barrier, inc=1, device_id={axis: lax.rem(here + k, size)}, device_id_type=MESH
+            )
+        count = count + size - 1
+    for axis, size in lines:
+        here = lax.axis_index(axis)
+
+        @pl.when(here > 0)
+        def _():
+            pl.semaphore_signal(barrier, inc=1, device_id={axis: here - 1}, device_id_type=MESH)
+
+        @pl.when(here < size - 1)
+        def _():
+            pl.semaphore_signal(barrier, inc=1, device_id={axis: here + 1}, device_id_type=MESH)
+
+        count = count + jnp.minimum(here, 1) + jnp.minimum(size - 1 - here, 1)
+    pl.semaphore_wait(barrier, count)
+
+
+class LineGather:
+    def __init__(self, size, pieces, src, dst, send, recv, local):
+        self.size, self.pieces, self.src, self.dst = size, pieces, src, dst
+        self.send, self.recv, self.local = send, recv, local
+        self.here = lax.axis_index("tp")
+        self.rows = src.shape[0] // pieces
+
+    def copy(self, way, hop, piece, shard, target):
+        rows = pl.ds(piece * self.rows, self.rows)
+        source = self.src.at[rows] if hop == 0 else self.dst.at[shard, rows]
+        return pltpu.make_async_remote_copy(
+            source, self.dst.at[shard, rows], self.send.at[way, hop, piece], self.recv.at[way, hop, piece],
+            device_id={"tp": target}, device_id_type=MESH,
+        )
+
+    def sent(self, way, hop):
+        if way == 0:
+            return (self.here - hop >= 0) & (self.here < self.size - 1), self.here - hop, self.here + 1
+        return (self.here + hop < self.size) & (self.here > 0), self.here + hop, self.here - 1
+
+    def arrived(self, way, hop):
+        if way == 0:
+            return self.here - 1 - hop >= 0, self.here - 1 - hop
+        return self.here + 1 + hop < self.size, self.here + 1 + hop
+
+    def start(self):
+        own = pltpu.make_async_copy(self.src, self.dst.at[self.here], self.local)
+        own.start()
+        for piece in range(self.pieces):
+            self.launch(0, piece)
+
+    def launch(self, hop, piece):
+        for way in range(2):
+            does, shard, target = self.sent(way, hop)
+
+            @pl.when(does)
+            def _():
+                self.copy(way, hop, piece, shard, target).start()
+
+    def take(self, hop, piece):
+        for way in range(2):
+            comes, shard = self.arrived(way, hop)
+
+            @pl.when(comes)
+            def _():
+                self.copy(way, hop, piece, shard, self.here).wait_recv()
+
+    def steps(self):
+        def forward(hop, piece):
+            self.take(hop - 1, piece)
+            self.launch(hop, piece)
+
+        return [partial(forward, hop, piece) for hop in range(1, self.size - 1) for piece in range(self.pieces)]
+
+    def finish(self):
+        for piece in range(self.pieces):
+            self.take(self.size - 2, piece)
+        for hop in range(self.size - 1):
+            for piece in range(self.pieces):
+                for way in range(2):
+                    does, shard, target = self.sent(way, hop)
+
+                    @pl.when(does)
+                    def _():
+                        self.copy(way, hop, piece, shard, target).wait_send()
+
+        pltpu.make_async_copy(self.src, self.dst.at[self.here], self.local).wait()
+
+
+def gather_scratch(size, pieces):
+    return [
+        pltpu.SemaphoreType.DMA((2, size - 1, pieces)), pltpu.SemaphoreType.DMA((2, size - 1, pieces)),
+        pltpu.SemaphoreType.DMA,
+    ]
+
+
+def spread(step, slot, slots, total, actions):
+    for place in range(total // slots):
+        due = [
+            act for i, act in enumerate(actions)
+            if (i + 1) * total // (len(actions) + 2) == place * slots + slot
+        ]
+        if due:
+            @pl.when(step == place)
+            def _():
+                for act in due:
+                    act()
+
+
+def first_gather_kernel(size, peers, pieces, x_ref, c_ref, small_ref, xs_ref, cs_ref, smalls_ref, *sems):
+    here = lax.axis_index("fsdp")
+    greet([("fsdp", peers)], [("tp", size)])
+    first = LineGather(size, pieces, x_ref.at[0], xs_ref, *sems[0:3])
+    second = LineGather(size, pieces, c_ref.at[0], cs_ref, *sems[3:6])
+    small_send, small_recv, small_local = sems[6:9]
+
+    def small_copy(k):
+        return pltpu.make_async_remote_copy(
+            small_ref, smalls_ref.at[here], small_send.at[k - 1], small_recv.at[k - 1],
+            device_id={"fsdp": lax.rem(here + k, peers)}, device_id_type=MESH,
+        )
+
+    def small_arrival(k):
+        origin = lax.rem(here + peers - k, peers)
+        return pltpu.make_async_remote_copy(
+            small_ref, smalls_ref.at[origin], small_send.at[k - 1], small_recv.at[k - 1],
+            device_id={"fsdp": origin}, device_id_type=MESH,
+        )
+
+    first.start()
+    second.start()
+    own = pltpu.make_async_copy(small_ref, smalls_ref.at[here], small_local)
+    own.start()
+    for k in range(1, peers):
+        small_copy(k).start()
+    own.wait()
+    for one, two in zip(first.steps(), second.steps()):
+        one()
+        two()
+    first.finish()
+    second.finish()
+    for k in range(1, peers):
+        small_arrival(k).wait_recv()
+        small_copy(k).wait_send()
+
+
+HBM = pl.BlockSpec(memory_space=pltpu.MemorySpace.HBM)
+
+
+def first_gather(size, peers, x, c, small):
+    _, rows, width = x.shape
+    pieces = 4
+    big = jax.ShapeDtypeStruct((size, rows, width), x.dtype)
+    xs, cs, smalls = pl.pallas_call(
+        partial(first_gather_kernel, size, peers, pieces),
+        in_specs=[HBM] * 3,
+        out_specs=[HBM] * 3,
+        out_shape=[big, big, jax.ShapeDtypeStruct((peers,) + small.shape, small.dtype)],
+        scratch_shapes=gather_scratch(size, pieces) * 2 + [
+            pltpu.SemaphoreType.DMA((peers - 1,)), pltpu.SemaphoreType.DMA((peers - 1,)), pltpu.SemaphoreType.DMA,
+        ],
+        compiler_params=pltpu.CompilerParams(collective_id=0, has_side_effects=True),
+        cost_estimate=pl.CostEstimate(flops=0, bytes_accessed=int(500e6), transcendentals=0),
+    )(x, c, small)
+    return xs.reshape(size * rows, width), cs.reshape(size * rows, width), smalls
+
+
+def attention_kernel(size, pieces, micro, row_tiles, heads, tile, *refs):
+    if micro is None:
+        return attention_body(row_tiles, heads, tile, *refs)
+    step = pl.program_id(0)
+    line = LineGather(size, pieces, refs[10].at[micro], refs[14], *refs[21:])
+
+    @pl.when(step == 0)
+    def _():
+        greet([], [("tp", size)])
+        line.start()
+
+    attention_body(row_tiles, heads, tile, *refs[:10], *refs[11:14], *refs[15:21])
+    spread(step, 0, 1, row_tiles + heads, line.steps())
+
+    @pl.when(step == row_tiles + heads - 1)
+    def _():
+        line.finish()
+
+
+def attention_body(
     row_tiles, heads, tile, len_ref, x_ref, c_ref, wqkv_ref, bqkv_ref, wo_ref, gain_ref, shift_ref,
     cos_ref, sin_ref, n1_ref, att_ref, gp_ref, q_s, k_s, v_s, ga_s, dk_s, dv_s,
 ):
@@ -121,32 +314,40 @@
     return pl.BlockSpec(shape, lambda i: (0,) * len(shape), pipeline_mode=pl.Buffered(1))
 
 
-def attention_call(length, x, c, wqkv, bqkv, wo, gain, shift, cos, sin):
+def attention_call(size, length, x, c, wqkv, bqkv, wo, gain, shift, cos, sin, ahead=None, micro=None):
     slot, width = x.shape
+    more = micro is not None
+    pieces = 2
+    gathered = jax.ShapeDtypeStruct((size, slot // size, width), BF16)
     heads = wqkv.shape[1] // (3 * HEAD)
     tile = 256
     row_tiles = slot // tile
     row_block = pl.BlockSpec((tile, width), lambda i: (jnp.minimum(i, row_tiles - 1), 0))
     head_at = lambda i: (0, jnp.maximum(i - row_tiles, 0))
-    return pl.pallas_call(
-        partial(attention_kernel, row_tiles, heads, tile),
+    out = pl.pallas_call(
+        partial(attention_kernel, size, pieces, micro, row_tiles, heads, tile),
         grid=(row_tiles + heads,),
         in_specs=[
             pl.BlockSpec(memory_space=pltpu.SMEM), row_block, row_block, whole(wqkv.shape), whole(bqkv.shape),
             whole(wo.shape), whole(gain.shape), whole(shift.shape), whole(cos.shape), whole(sin.shape),
-        ],
-        out_specs=[row_block, pl.BlockSpec((slot, HEAD), head_at), pl.BlockSpec((slot, 3 * HEAD), head_at)],
+        ] + [HBM] * more,
+        out_specs=[
+            row_block, pl.BlockSpec((slot, HEAD), head_at), pl.BlockSpec((slot, 3 * HEAD), head_at)
+        ] + [HBM] * more,
         out_shape=[
             jax.ShapeDtypeStruct((slot, width), BF16),
             jax.ShapeDtypeStruct((slot, heads * HEAD), BF16),
             jax.ShapeDtypeStruct((slot, heads * 3 * HEAD), BF16),
-        ],
-        scratch_shapes=[pltpu.VMEM((heads, slot, HEAD), BF16)] * 4 + [pltpu.VMEM((slot, HEAD), F32)] * 2,
+        ] + [gathered] * more,
+        scratch_shapes=[pltpu.VMEM((heads, slot, HEAD), BF16)] * 4 + [pltpu.VMEM((slot, HEAD), F32)] * 2
+        + (gather_scratch(size, pieces) if more else []),
         compiler_params=pltpu.CompilerParams(
-            dimension_semantics=("arbitrary",), vmem_limit_bytes=VMEM_BYTES
+            dimension_semantics=("arbitrary",), vmem_limit_bytes=VMEM_BYTES,
+            **(dict(collective_id=1, has_side_effects=True) if more else {}),
         ),
         cost_estimate=pl.CostEstimate(flops=int(14e9), bytes_accessed=int(20e6), transcendentals=int(3e6)),
-    )(length, x, c, wqkv, bqkv, wo, gain, shift, cos, sin)
+    )(length, x, c, wqkv, bqkv, wo, gain, shift, cos, sin, *([ahead] if more else []))
+    return (*out[:3], out[3].reshape(slot, width) if more else None)
 
 
 def normal_pair(value):
@@ -157,8 +358,28 @@
     return jnp.where(value >= 0, 1.0 - tail, tail), density * (1.0 / math.sqrt(2.0 * math.pi))
 
 
-def feed_kernel(
-    tile, chunk, len_ref, x_ref, c_ref, att_ref, gp_ref, w1_ref, w2_ref, wo_ref, wqkv_ref, b1_ref,
+def feed_kernel(size, pieces, micro, tile, chunk, steps, *refs):
+    if micro is None:
+        return feed_body(lambda slot: None, tile, chunk, *refs)
+    step = pl.program_id(0)
+    line = LineGather(size, pieces, refs[13].at[micro], refs[22], *refs[25:])
+
+    @pl.when(step == 0)
+    def _():
+        greet([], [("tp", size)])
+        line.start()
+
+    feed_body(
+        lambda slot: spread(step, slot, 4, 4 * steps, line.steps()), tile, chunk, *refs[:13], *refs[14:22], *refs[23:25]
+    )
+
+    @pl.when(step == steps - 1)
+    def _():
+        line.finish()
+
+
+def feed_body(
+    hook, tile, chunk, len_ref, x_ref, c_ref, att_ref, gp_ref, w1_ref, w2_ref, wo_ref, wqkv_ref, b1_ref,
     gain1_ref, gain2_ref, shift2_ref, n2_ref, act_ref, gpre_ref, h_ref, u_ref, sd_ref, sf_ref, sq_ref, xhat_s, cot_s,
 ):
     step = pl.program_id(0)
@@ -189,10 +410,14 @@
         gpre = (gact * (below + pre * density)).astype(BF16)
         gpre_ref[:, cols] = gpre
         sf_ref[:, cols] += dot_nn(ones, gpre)
+        if k == hidden // chunk // 2 - 1:
+            hook(0)
+    hook(1)
     sq_ref[...] += dot_nn(ones, gp_ref[...])
     for j in range(blocks):
         cols = slice(j * width, (j + 1) * width)
         h_ref[:, cols] = (dot_nn(act_ref[...], w2_ref[j]) + dot_nn(att_ref[...], wo_ref[j])).astype(BF16)
+    hook(2)
     for k in range(model // chunk):
         cols = slice(k * chunk, (k + 1) * chunk)
         g2 = dot_nt(gpre_ref[...], w1_ref[cols, :])
@@ -204,28 +429,32 @@
         sd_ref[2:3, cols] += jnp.sum(g2 * hat, axis=0, keepdims=True)
         sd_ref[3:4, cols] += jnp.sum(g2, axis=0, keepdims=True)
         sd_ref[4:5, cols] += dot_nn(ones, cot_s[:, cols])[0:1]
-
-
-def feed_call(length, x, c, att, gp, w1, w2, wo, wqkv, b1, gain1, gain2, shift2):
+    hook(3)
+
+
+def feed_call(size, length, x, c, att, gp, w1, w2, wo, wqkv, b1, gain1, gain2, shift2, ahead=None, micro=None):
     slot, width = x.shape
+    more = micro is not None
+    pieces = 2
+    gathered = jax.ShapeDtypeStruct((size, slot // size, width), BF16)
     hidden = w1.shape[1]
     tile, chunk = 256, 512
     at = lambda i: (i, 0)
     keep = lambda i: (0, 0)
     row_block = pl.BlockSpec((tile, width), at)
     hid_block = pl.BlockSpec((tile, hidden), at)
-    return pl.pallas_call(
-        partial(feed_kernel, tile, chunk),
+    out = pl.pallas_call(
+        partial(feed_kernel, size, pieces, micro, tile, chunk, slot // tile),
         grid=(slot // tile,),
         in_specs=[
             pl.BlockSpec(memory_space=pltpu.SMEM), row_block, row_block, pl.BlockSpec((tile, att.shape[1]), at),
             pl.BlockSpec((tile, gp.shape[1]), at), whole(w1.shape), whole(w2.shape), whole(wo.shape),
             whole(wqkv.shape), whole(b1.shape), whole(gain1.shape), whole(gain2.shape), whole(shift2.shape),
-        ],
+        ] + [HBM] * more,
         out_specs=[
             row_block, hid_block, hid_block, row_block, row_block,
             pl.BlockSpec((8, width), keep), pl.BlockSpec((8, hidden), keep), pl.BlockSpec((8, gp.shape[1]), keep),
-        ],
+        ] + [HBM] * more,
         out_shape=[
             jax.ShapeDtypeStruct((slot, width), BF16),
             jax.ShapeDtypeStruct((slot, hidden), BF16),
@@ -235,13 +464,16 @@
             jax.ShapeDtypeStruct((8, width), F32),
             jax.ShapeDtypeStruct((8, hidden), F32),
             jax.ShapeDtypeStruct((8, gp.shape[1]), F32),
-        ],
-        scratch_shapes=[pltpu.VMEM((tile, width), F32), pltpu.VMEM((tile, width), BF16)],
+        ] + [gathered] * more,
+        scratch_shapes=[pltpu.VMEM((tile, width), F32), pltpu.VMEM((tile, width), BF16)]
+        + (gather_scratch(size, pieces) if more else []),
         compiler_params=pltpu.CompilerParams(
-            dimension_semantics=("arbitrary",), vmem_limit_bytes=VMEM_BYTES
+            dimension_semantics=("arbitrary",), vmem_limit_bytes=VMEM_BYTES,
+            **(dict(collective_id=2, has_side_effects=True) if more else {}),
         ),
         cost_estimate=pl.CostEstimate(flops=int(45e9), bytes_accessed=int(50e6), transcendentals=int(4e6)),
-    )(length, x, c, att, gp, w1, w2, wo, wqkv, b1, gain1, gain2, shift2)
+    )(length, x, c, att, gp, w1, w2, wo, wqkv, b1, gain1, gain2, shift2, *([ahead] if more else []))
+    return (*out[:8], out[8].reshape(slot, width) if more else None)
 
 
 def shards(
@@ -258,7 +490,12 @@
     gather = lambda value, axis: lax.all_gather(value, axis, axis=0, tiled=True)
 
     small = (qkv_bias, fc1_bias, out_bias, fc2_bias, ln1_gain, ln1_bias, ln2_gain, ln2_bias)
-    packed = lax.all_gather(jnp.concatenate(small), "fsdp", axis=0, tiled=False).astype(F32)
+    flat = jnp.concatenate(small).astype(F32)
+    lines = 8 * 128
+    flat = jnp.pad(flat, (0, -flat.shape[0] % lines)).reshape(8, -1)
+    peers = lax.axis_size("fsdp")
+    x, c, packed = first_gather(tp_size, peers, hidden_in, out_grad, flat)
+    packed = packed.reshape(peers, -1)
     rows, start = [], 0
     for value in small:
         rows.append(packed[:, start:start + value.shape[0]].reshape(1, -1))
@@ -272,11 +509,13 @@
     parts, outputs, in_grads = [], [], []
     for m in range(micro_count):
         length = lengths[m]
-        x = gather(hidden_in[m], "tp")
-        c = gather(out_grad[m], "tp")
-        n1, att, gp = attention_call(length, x, c, wqkv, bqkv, wo, gain1, shift1, cos, sin)
-        n2, act, gpre, h, u, sd, sf, sq = feed_call(
-            length, x, c, att, gp, w1, w2, wo, wqkv, b1, gain1, gain2, shift2
+        ahead = dict(ahead=hidden_in, micro=m + 1) if m + 1 < micro_count else {}
+        n1, att, gp, x_next = attention_call(
+            tp_size, length, x, c, wqkv, bqkv, wo, gain1, shift1, cos, sin, **ahead
+        )
+        ahead = dict(ahead=out_grad, micro=m + 1) if m + 1 < micro_count else {}
+        n2, act, gpre, h, u, sd, sf, sq, c_next = feed_call(
+            tp_size, length, x, c, att, gp, w1, w2, wo, wqkv, b1, gain1, gain2, shift2, **ahead
         )
         valid = (jnp.arange(slot) < length[0])[:, None]
         cot = jnp.where(valid, c, jnp.zeros_like(c))
@@ -293,6 +532,7 @@
             - xhat * jnp.mean(u_own * xhat, axis=-1, keepdims=True)
         )
         in_grads.append((jnp.where(live, out_grad[m].astype(F32), 0.0) + back).astype(BF16))
+        x, c = x_next, c_next
 
     def weight_grad(left, right):
         total = dot_tn(parts[0][left], parts[0][right])

time: 1120 us -> 985 us (0.88)
  waiting for transfers between devices: 680 us -> 363 us
  Pallas kernels: 217 us -> 431 us
  blocking collectives: 61.9 us -> 35.7 us
    all_gather x6 -> x2, waiting for transfers between devices: 317 us -> 0.01 us  [shards(): gather = lambda value, axis: lax.all_gather(value, axis, axis=0, tiled=True)]
    pallas_call x4 -> x5, Pallas kernels: 217 us -> 431 us  [the longest x1 163 us: first_gather(): pl.pallas_call(partial(first_gather_kernel, size, peers, pieces), in_spec...]
    reduce_scatter x4, waiting for transfers between devices: 138 us -> 201 us  [weight_grad(): lax.psum_scatter(total.astype(BF16), 'fsdp', scatter_dimension=0, tiled=T...]
    all_gather x1, waiting for transfers between devices: 42.6 us -> 0.01 us  [shards(): w2 = lax.all_gather(fc2_weight, 'fsdp', axis=0, tiled=False)]
    unnamed x1 -> x0, blocking collectives: 25.8 us -> none
    reduce_scatter x2, waiting for transfers between devices: 97.1 us -> 79.6 us  [shards(): h_own = lax.psum_scatter(h, 'tp', scatter_dimension=0, tiled=True)]
  transfers between devices with their start and end apart: 16 -> 12, of which waited for: 11 -> 5; matrix products, arithmetic and copies ran while one was open for 12% -> 13% of each run, Pallas kernels for 19% -> 31%
where the time goes in v2:
time: 985 us; the launch traced here: 981 us
  Pallas kernels  431 us (44%)
  waiting for transfers between devices  363 us (37%)
  matrix products  96.2 us (10%)
  blocking collectives  35.7 us (4%)
  other arithmetic  27.1 us (3%)
  between operations  15 us (2%)
  local copies, waits for them, and re-layouts  12.8 us (1%)
    reduce_scatter x4, waiting for transfers between devices, weight_grad(): lax.psum_scatter(total.astype(BF16), 'fsdp', scatter_dimension=0, tiled=T...  201 us
    pallas_call x1, Pallas kernels, first_gather(): pl.pallas_call(partial(first_gather_kernel, size, peers, pieces), in_spec...  163 us
    pallas_call x2, Pallas kernels, feed_call(): pl.pallas_call(partial(feed_kernel, size, pieces, micro, tile, chunk, slo...  152 us
    pallas_call x2, Pallas kernels, attention_call(): pl.pallas_call(partial(attention_kernel, size, pieces, micro, row_tiles,...  116 us
    dot_general x8, matrix products, dot_tn(): lax.dot_general(a, b, (((0,), (0,)), ((), ())), preferred_element_type=F32)  96.2 us
    reduce_scatter x2, waiting for transfers between devices, shards(): h_own = lax.psum_scatter(h, 'tp', scatter_dimension=0, tiled=True)  79.6 us
    reduce_scatter x2, waiting for transfers between devices, shards(): lax.psum_scatter(u, 'tp', scatter_dimension=0, tiled=True).astype(F32)  77.9 us
    psum x1, blocking collectives, shards(): lax.psum(jnp.concatenate([sums[0][:5].reshape(-1), sums[1][0], sums[2][0]...  24.3 us
  transfers between devices with their start and end apart: 12, of which 5 were waited for; matrix products, arithmetic and copies ran while one was open for 13% of the time, Pallas kernels for 31%

profile of v2, /device:TPU:0, one launch (start us, length us, event | category | flops | bytes accessed | tf_op | source)
XLA Modules:
  0.0 981.0 jit_solution(10096102710285615370)
XLA Ops:
  10.9 162.6 %shard_map.254 = (bf16[4,256,2048]{2,1,0:T(8,128)(2,1)}, bf16[4,256,2048]{2,1,0:T(8,128)(2,1)}, f32[8,8,256]{2,1,0:T(8,128)}) custom-call(bf16[2,256,2048]{2,1,0:T(8,128)(2,1)} %refs_10_.1, bf16[2,256,2048]{2,1,0:T(8,128)(2,1)} %refs_13_.1, f32[8,256]{1,0:T(8,128)} %reshape.166.small_ref), custom_call_target="tpu_custom_call" | custom-call | bytes 500000000 | tf_op jit(solution)/shard_map/pallas_call | solution.py:219
  180.8 1.9 fusion.36
  182.8 1.3 maximum_maximum_fusion
  184.1 76.9 %shard_map.255 = (bf16[1024,2048]{1,0:T(8,128)(2,1)}, bf16[1024,512]{1,0:T(8,128)(2,1)}, bf16[1024,1536]{1,0:T(8,128)(2,1)}, bf16[4,256,2048]{2,1,0:T(8,128)(2,1)}) custom-call(s32[1]{0:T(128)} %bitcast.2.refs_0_, bf16[1024,2048]{1,0:T(8,128)(2,1)} %bitcast.180, bf16[1024,2048]{1,0:T(8,128)(2,1)} %bitcast.176, ...), custom_call_target="tpu_custom_call" | custom-call | flops 14000000000 | bytes 20000000 | tf_op jit(solution)/shard_map/pallas_call | solution.py:327
  261.0 7.1 fusion.31
  268.0 82.1 %shard_map.256 = (bf16[1024,2048]{1,0:T(8,128)(2,1)}, bf16[1024,2048]{1,0:T(8,128)(2,1)}, bf16[1024,2048]{1,0:T(8,128)(2,1)}, bf16[1024,2048]{1,0:T(8,128)(2,1)}...) custom-call(s32[1]{0:T(128)} %bitcast.2.refs_0_, ...), custom_call_target="tpu_custom_call" | custom-call | flops 44999999488 | bytes 50000000 | tf_op jit(solution)/shard_map/pallas_call | solution.py:446
  350.1 39.4 %shard_map.257 = (bf16[1024,2048]{1,0:T(8,128)(2,1)}, bf16[1024,512]{1,0:T(8,128)(2,1)}, bf16[1024,1536]{1,0:T(8,128)(2,1)}) custom-call(s32[1]{0:T(128)} %bitcast.10.refs_0_, bf16[1024,2048]{1,0:T(8,128)(2,1)} %bitcast.190, bf16[1024,2048]{1,0:T(8,128)(2,1)} %bitcast.186, bf16[2048,1536]{1,0:T(8,128)(2,1)} %all-gather.7.cloned.1.call-done.refs_3_.refs_8_, ...), custom_call_target="tpu_custom_call" | custom-call | flops 14000000000 | bytes 20000000 | tf_op jit(solution)/shard_map/pallas_call | solution.py:327
  389.6 7.7 add_convert_fusion.3
  397.9 69.6 %shard_map.258 = (bf16[1024,2048]{1,0:T(8,128)(2,1)}, bf16[1024,2048]{1,0:T(8,128)(2,1)}, bf16[1024,2048]{1,0:T(8,128)(2,1)}, bf16[1024,2048]{1,0:T(8,128)(2,1)}...) custom-call(s32[1]{0:T(128)} %bitcast.10.refs_0_, ...), custom_call_target="tpu_custom_call" | custom-call | flops 44999999488 | bytes 50000000 | tf_op jit(solution)/shard_map/pallas_call | solution.py:446
  469.0 9.9 %fusion.46 = f32[2048,1536]{1,0:T(8,128)S(1)} fusion(bf16[1024,2048]{1,0:T(8,128)(2,1)} %get-tuple-element.54, bf16[1024,1536]{1,0:T(8,128)(2,1)} %get-tuple-element.45.refs_4_), kind=kOutput, calls=%fused_computation.98 | convolution fusion | flops 6442450944 | bytes 19922944 | tf_op jit(solution)/shard_map/dot_general | solution.py:29
  478.9 9.2 add_convert_fusion.2
  488.2 16.1 %fusion.30 = f32[2048,2048]{1,0:T(8,128)} fusion(bf16[1024,2048]{1,0:T(8,128)(2,1)} %get-tuple-element.66, bf16[1024,2048]{1,0:T(8,128)(2,1)} %bitcast.179, pred[1024]{0:T(1024)(128)(4,1)S(1)} %iota_compare_fusion.1), kind=kOutput, calls=%fused_computation.51 | convolution fusion | flops 8592031744 | bytes 25166848 | tf_op jit(solution)/shard_map/dot_general | solution.py:29
  504.4 16.0 %add_convert_fusion = bf16[2048,2048]{1,0:T(8,128)(2,1)} fusion(f32[2048,2048]{1,0:T(8,128)} %fusion.30, bf16[1024,2048]{1,0:T(8,128)(2,1)} %get-tuple-element.67, bf16[1024,2048]{1,0:T(8,128)(2,1)S(1)} %bitcast.189, pred[1024]{0:T(1024)(128)(4,1)S(1)} %iota_compare_fusion), kind=kOutput, calls=%fused_computation | convolution fusion | flops 8600420352 | bytes 33555456 | tf_op jit(solution)/shard_map/dot_general | solution.py:29
  520.5 15.5 %fusion.47 = f32[2048,2048]{1,0:T(8,128)} fusion(bf16[1024,2048]{1,0:T(8,128)(2,1)} %get-tuple-element.62, bf16[1024,2048]{1,0:T(8,128)(2,1)} %get-tuple-element.63), kind=kOutput, calls=%fused_computation.99 | convolution fusion | flops 8589934592 | bytes 25165824 | tf_op jit(solution)/shard_map/dot_general | solution.py:29
  536.0 14.7 %add_convert_fusion.1 = bf16[2048,2048]{1,0:T(8,128)(2,1)} fusion(f32[2048,2048]{1,0:T(8,128)} %fusion.47, bf16[1024,2048]{1,0:T(8,128)(2,1)S(1)} %copy-done.21, bf16[1024,2048]{1,0:T(8,128)(2,1)S(1)} %copy-done.22), kind=kOutput, calls=%fused_computation.1 | convolution fusion | flops 8598323200 | bytes 33554432 | tf_op jit(solution)/shard_map/dot_general | solution.py:29
  555.3 24.3 %psum.14 = f32[13824]{0:T(1024)S(1)} all-reduce(f32[13824]{0:T(1024)S(1)} %pad_maximum_fusion.2), channel_id=1, replica_groups=mesh['fsdp'=8,'tp'=4] {'fsdp'}, use_global_device_ids=true, to_apply=%region_13.14 | all-reduce | flops 13824 | bytes 110592 | tf_op jit(solution)/shard_map/psum | solution.py:548
  581.1 11.3 %psum.15 = f32[4,256]{1,0:T(4,128)S(1)} all-reduce(f32[4,256]{1,0:T(4,128)S(1)} %constant_dynamic-slice_fusion), channel_id=1, replica_groups=mesh['fsdp'=8,'tp'=4] {'tp'}, use_global_device_ids=true, to_apply=%region_17.18 | all-reduce | flops 1024 | bytes 8192 | tf_op jit(solution)/shard_map/psum | solution.py:553
  593.0 1.0 convert_bitcast_fusion.3
  595.0 2.3 fusion.28
  597.4 77.9 %reduce-scatter.15.cloned.1.call-done = bf16[256,2048]{1,0:T(8,128)(2,1)} async-done(((bf16[1024,2048]{1,0:T(8,128)(2,1)}), bf16[256,2048]{1,0:T(8,128)(2,1)}) %reduce-scatter.15.cloned.1.call-update) | async-done | bytes 1048592 | tf_op jit(solution)/shard_map/reduce_scatter | solution.py:524
  675.3 79.6 %reduce-scatter.9.cloned.1.call-done = bf16[256,2048]{1,0:T(8,128)(2,1)} async-done(((bf16[1024,2048]{1,0:T(8,128)(2,1)}), bf16[256,2048]{1,0:T(8,128)(2,1)}) %reduce-scatter.9.cloned.1.call-update) | async-done | bytes 1048592 | tf_op jit(solution)/shard_map/reduce_scatter | solution.py:523
  754.9 3.6 convert_reduce_fusion
  758.6 2.1 fusion.35
  760.7 1.5 pad_maximum_fusion.1
  762.2 1.5 pad_maximum_fusion
  763.7 57.1 %reduce-scatter.17.cloned.1.call-done = bf16[256,1536]{1,0:T(8,128)(2,1)} async-done(((bf16[2048,1536]{1,0:T(8,128)(2,1)}), bf16[256,1536]{1,0:T(8,128)(2,1)}) %reduce-scatter.17.cloned.1.call-update) | async-done | bytes 786448 | tf_op jit(solution)/shard_map/reduce_scatter | solution.py:541
  820.8 2.5 convert_element_type.116
  823.3 72.3 %reduce-scatter.23.cloned.1.call-done = bf16[256,2048]{1,0:T(8,128)(2,1)} async-done(((bf16[2048,2048]{1,0:T(8,128)(2,1)}), bf16[256,2048]{1,0:T(8,128)(2,1)}) %reduce-scatter.23.cloned.1.call-update) | async-done | bytes 1048592 | tf_op jit(solution)/shard_map/reduce_scatter | solution.py:541
  895.6 1.5 convert_bitcast_fusion.2
  897.0 1.8 copy.33
  898.8 71.8 %reduce-scatter.21.cloned.1.call-done = bf16[256,2048]{1,0:T(8,128)(2,1)} async-done(((bf16[2048,2048]{1,0:T(8,128)(2,1)}), bf16[256,2048]{1,0:T(8,128)(2,1)}) %reduce-scatter.21.cloned.1.call-update) | async-done | bytes 1048592 | tf_op jit(solution)/shard_map/reduce_scatter | solution.py:541
  970.6 2.8 convert_element_type.119
  (127 shorter events, 21.2 us)
Async XLA Ops:
  7.2 2.9 copy-start.10
  7.2 2.9 copy-start.12
  7.2 2.9 copy-start.11
  7.2 2.9 copy-start.13
  7.2 2.9 copy-start.14
  7.2 2.9 copy-start.15
  7.2 2.9 copy-start.16
  7.3 2.9 copy-start.17
  7.3 176.8 %all-gather.11.cloned.1.call-start = ((), (), s32[]{:S(2)}) async-start(), calls=%async_computation.18 | async-start | bytes 2359296 | tf_op jit(solution)/shard_map/all_gather | solution.py:505
  8.0 176.1 %all-gather.7.cloned.1.call-start = ((), (), s32[]{:S(2)}) async-start(), calls=%async_computation.8 | async-start | bytes 7077888 | tf_op jit(solution)/shard_map/all_gather | solution.py:490
  8.7 170.2 %copy-start.9 = (s32[2,1]{0,1:T(1,128)S(1)}, s32[2,1]{0,1:T(1,128)}, u32[]{:S(2)}) copy-start(s32[2,1]{0,1:T(1,128)} %param.17) | copy-start | bytes 28
  8.8 259.3 %all-gather.9.cloned.1.call-start = ((), (), s32[]{:S(2)}) async-start(), calls=%async_computation.9 | async-start | bytes 9437184 | tf_op jit(solution)/shard_map/all_gather | solution.py:490
  9.5 258.5 %all-gather.13.cloned.1.call-start = ((), (), s32[]{:S(2)}) async-start(), calls=%async_computation.19 | async-start | bytes 9437184 | tf_op jit(solution)/shard_map/all_gather | solution.py:507
  10.1 582.9 %reduce-scatter.19.cloned.1.call-start = ((), (), s32[]{:S(2)}) async-start(), calls=%async_computation.15 | async-start | bytes 2359296 | tf_op jit(solution)/shard_map/reduce_scatter | solution.py:541
  397.3 197.7 %reduce-scatter.13.cloned.1.call-start = ((), (), s32[]{:S(2)}) async-start(), calls=%async_computation.12 | async-start | bytes 5242880 | tf_op jit(solution)/shard_map/reduce_scatter | solution.py:524
  397.8 199.5 %reduce-scatter.11.cloned.1.call-start = ((), (), s32[]{:S(2)}) async-start(), calls=%async_computation.11 | async-start | bytes 5242880 | tf_op jit(solution)/shard_map/reduce_scatter | solution.py:523
  467.5 207.9 %reduce-scatter.15.cloned.1.call-start = ((), (), s32[]{:S(2)}) async-start(), calls=%async_computation.13 | async-start | bytes 5242880 | tf_op jit(solution)/shard_map/reduce_scatter | solution.py:524
  468.2 286.7 %reduce-scatter.9.cloned.1.call-start = ((), (), s32[]{:S(2)}) async-start(), calls=%async_computation.10 | async-start | bytes 5242880 | tf_op jit(solution)/shard_map/reduce_scatter | solution.py:523
  468.9 351.9 %reduce-scatter.17.cloned.1.call-start = ((), (), s32[]{:S(2)}) async-start(), calls=%async_computation.14 | async-start | bytes 7077888 | tf_op jit(solution)/shard_map/reduce_scatter | solution.py:541
  469.0 9.9 %copy-start.19 = (bf16[1024,2048]{1,0:T(8,128)(2,1)S(1)}, bf16[1024,2048]{1,0:T(8,128)(2,1)}, u32[]{:S(2)}) copy-start(bf16[1024,2048]{1,0:T(8,128)(2,1)} %get-tuple-element.55) | copy-start | bytes 12582916
  469.0 9.9 %copy-start.20 = (bf16[1024,1536]{1,0:T(8,128)(2,1)S(1)}, bf16[1024,1536]{1,0:T(8,128)(2,1)}, u32[]{:S(2)}) copy-start(bf16[1024,1536]{1,0:T(8,128)(2,1)} %get-tuple-element.50.refs_4_) | copy-start | bytes 9437188
  488.2 407.4 %reduce-scatter.23.cloned.1.call-start = ((), (), s32[]{:S(2)}) async-start(), calls=%async_computation.17 | async-start | bytes 9437184 | tf_op jit(solution)/shard_map/reduce_scatter | solution.py:541
  488.2 16.2 %copy-start.18 = (bf16[4,256,2048]{2,1,0:T(8,128)(2,1)S(1)}, bf16[4,256,2048]{2,1,0:T(8,128)(2,1)}, u32[]{:S(2)}) copy-start(bf16[4,256,2048]{2,1,0:T(8,128)(2,1)} %get-tuple-element.48) | copy-start | bytes 12582916
  520.4 450.2 %reduce-scatter.21.cloned.1.call-start = ((), (), s32[]{:S(2)}) async-start(), calls=%async_computation.16 | async-start | bytes 9437184 | tf_op jit(solution)/shard_map/reduce_scatter | solution.py:541
  520.4 15.6 %copy-start.21 = (bf16[1024,2048]{1,0:T(8,128)(2,1)S(1)}, bf16[1024,2048]{1,0:T(8,128)(2,1)}, u32[]{:S(2)}) copy-start(bf16[1024,2048]{1,0:T(8,128)(2,1)} %get-tuple-element.64) | copy-start | bytes 12582916
  520.4 15.6 %copy-start.22 = (bf16[1024,2048]{1,0:T(8,128)(2,1)S(1)}, bf16[1024,2048]{1,0:T(8,128)(2,1)}, u32[]{:S(2)}) copy-start(bf16[1024,2048]{1,0:T(8,128)(2,1)} %get-tuple-element.65) | copy-start | bytes 12582916
  550.7 2.8 copy-start.4
  550.7 2.8 copy-start.5
  579.8 393.6 %copy-start.8 = (f32[1,256]{1,0:T(1,128)}, f32[1,256]{1,0:T(1,128)S(1)}, u32[]{:S(2)}) copy-start(f32[1,256]{1,0:T(1,128)S(1)} %dynamic-slice) | copy-start | bytes 3076
  754.9 3.7 copy-start.1
  754.9 3.7 copy-start.2
  754.9 3.7 copy-start.3
  (3 other events, 3.4 us)
Sparse Core Ops, SparseCore 0:
  10.0 30.5 all-gather.10
  42.5 45.5 all-gather.6
  89.9 54.3 all-gather.8
  146.1 54.3 all-gather.12
  397.4 39.3 reduce-scatter.18
  439.0 76.7 reduce-scatter.12
  518.1 77.5 reduce-scatter.10
  598.0 77.2 reduce-scatter.14
  677.6 77.2 reduce-scatter.8
  758.5 62.2 reduce-scatter.16
  824.3 71.2 reduce-scatter.22
  899.3 71.2 reduce-scatter.20

commit v3 on v2

v3 whole, which is shorter than its diff:
```python
from functools import partial
import math

import jax
import jax.numpy as jnp
import numpy as np
from jax import lax
from jax.experimental import pallas as pl
from jax.experimental.pallas import tpu as pltpu
from jax.sharding import PartitionSpec as P

HEAD = 128
ROT = 32
EPSILON = 1e-05
MASKED = -1e30
F32 = jnp.float32
BF16 = jnp.bfloat16
VMEM_BYTES = 60 << 20


def dot_nn(a, b):
    return lax.dot_general(a, b, (((1,), (0,)), ((), ())), preferred_element_type=F32)


def dot_nt(a, b):
    return lax.dot_general(a, b, (((1,), (1,)), ((), ())), preferred_element_type=F32)


def dot_tn(a, b):
    return lax.dot_general(a, b, (((0,), (0,)), ((), ())), preferred_element_type=F32)


def row_stats(rows):
    mean = jnp.mean(rows, axis=-1, keepdims=True)
    centred = rows - mean
    spread = jnp.mean(centred * centred, axis=-1, keepdims=True)
    rstd = lax.rsqrt(spread + EPSILON)
    return centred * rstd, rstd


def rotary_full(row_count):
    exponent = np.arange(0, ROT, 2, dtype=np.float32) / np.float32(ROT)
    inverse = (1.0 / 10000.0 ** exponent.astype(np.float64)).astype(np.float32)
    angles = (np.arange(row_count, dtype=np.float32)[:, None] * inverse[None, :]).astype(np.float64)
    cosine, sine = np.cos(angles).astype(np.float32), np.sin(angles).astype(np.float32)
    rest = np.ones((row_count, HEAD - ROT), np.float32)
    return (
        jnp.asarray(np.concatenate([cosine, cosine, rest], axis=1)),
        jnp.asarray(np.concatenate([-sine, sine, 0.0 * rest], axis=1)),
    )


def swap_halves(block):
    half = ROT // 2
    lane = lax.broadcasted_iota(jnp.int32, block.shape, 1)
    return jnp.where(lane < half, pltpu.roll(block, HEAD - half, 1), pltpu.roll(block, half, 1))

MESH = pl.DeviceIdType.MESH


def greet(axes, lines):
    barrier = pltpu.get_barrier_semaphore()
    count = 0
    for axis, size in axes:
        here = lax.axis_index(axis)
        for k in range(1, size):
            pl.semaphore_signal(
                barrier, inc=1, device_id={axis: lax.rem(here + k, size)}, device_id_type=MESH
            )
        count = count + size - 1
    for axis, size in lines:
        here = lax.axis_index(axis)

        @pl.when(here > 0)
        def _():
            pl.semaphore_signal(barrier, inc=1, device_id={axis: here - 1}, device_id_type=MESH)

        @pl.when(here < size - 1)
        def _():
            pl.semaphore_signal(barrier, inc=1, device_id={axis: here + 1}, device_id_type=MESH)

        count = count + jnp.minimum(here, 1) + jnp.minimum(size - 1 - here, 1)
    pl.semaphore_wait(barrier, count)


class LineGather:
    def __init__(self, size, pieces, src, dst, send, recv, local):
        self.size, self.pieces, self.src, self.dst = size, pieces, src, dst
        self.send, self.recv, self.local = send, recv, local
        self.here = lax.axis_index("tp")
        self.rows = src.shape[0] // pieces
        self.settled = False

    def copy(self, way, hop, piece, shard, target):
        rows = pl.ds(piece * self.rows, self.rows)
        source = self.src.at[rows] if hop == 0 else self.dst.at[shard, rows]
        return pltpu.make_async_remote_copy(
            source, self.dst.at[shard, rows], self.send.at[way, hop, piece], self.recv.at[way, hop, piece],
            device_id={"tp": target}, device_id_type=MESH,
        )

    def sent(self, way, hop):
        if way == 0:
            return (self.here - hop >= 0) & (self.here < self.size - 1), self.here - hop, self.here + 1
        return (self.here + hop < self.size) & (self.here > 0), self.here + hop, self.here - 1

    def arrived(self, way, hop):
        if way == 0:
            return self.here - 1 - hop >= 0, self.here - 1 - hop
        return self.here + 1 + hop < self.size, self.here + 1 + hop

    def start(self):
        own = pltpu.make_async_copy(self.src, self.dst.at[self.here], self.local)
        own.start()
        for piece in range(self.pieces):
            self.launch(0, piece)

    def launch(self, hop, piece):
        for way in range(2):
            does, shard, target = self.sent(way, hop)

            @pl.when(does)
            def _():
                self.copy(way, hop, piece, shard, target).start()

    def take(self, hop, piece):
        for way in range(2):
            comes, shard = self.arrived(way, hop)

            @pl.when(comes)
            def _():
                self.copy(way, hop, piece, shard, self.here).wait_recv()

    def steps(self):
        def forward(hop, piece):
            self.take(hop - 1, piece)
            self.launch(hop, piece)

        return [partial(forward, hop, piece) for hop in range(1, self.size - 1) for piece in range(self.pieces)]

    def finish(self, taken=False):
        if not taken:
            for piece in range(self.pieces):
                self.take(self.size - 2, piece)
        for hop in range(self.size - 1):
            for piece in range(self.pieces):
                for way in range(2):
                    does, shard, target = self.sent(way, hop)

                    @pl.when(does)
                    def _():
                        self.copy(way, hop, piece, shard, target).wait_send()

        if not self.settled:
            self.settle()

    def settle(self):
        self.settled = True
        pltpu.make_async_copy(self.src, self.dst.at[self.here], self.local).wait()

    def order(self, j):
        both = jnp.minimum(self.here, self.size - 1 - self.here)
        near = self.here + jnp.where(lax.rem(j, 2) == 0, j // 2, -((j + 1) // 2))
        rest = jnp.where(self.here < self.size - 1 - self.here, j, self.size - 1 - j)
        return jnp.where(j <= 2 * both, near, rest)


def gather_scratch(size, pieces):
    return [
        pltpu.SemaphoreType.DMA((2, size - 1, pieces)), pltpu.SemaphoreType.DMA((2, size - 1, pieces)),
        pltpu.SemaphoreType.DMA,
    ]


class PlaneGather:
    def __init__(self, peers, src, dst, send, recv, pass_send, pass_recv, local):
        self.chips, self.src, self.dst = peers // 2, src, dst
        self.send, self.recv, self.pass_send, self.pass_recv, self.local = send, recv, pass_send, pass_recv, local
        self.here = lax.axis_index("fsdp")
        self.chip, self.core = self.here // 2, lax.rem(self.here, 2)

    def far(self, s, origin):
        return pltpu.make_async_remote_copy(
            self.src, self.dst.at[origin], self.send.at[s], self.recv.at[s],
            device_id={"fsdp": 2 * lax.rem(self.chip + s, self.chips) + self.core}, device_id_type=MESH,
        )

    def origin(self, s, core):
        return 2 * lax.rem(self.chip + self.chips - s, self.chips) + core

    def near(self, s, core):
        shard = self.origin(s, core)
        return pltpu.make_async_remote_copy(
            self.src if s == 0 else self.dst.at[shard], self.dst.at[shard], self.pass_send.at[s], self.pass_recv.at[s],
            device_id={"fsdp": 2 * self.chip + 1 - self.core}, device_id_type=MESH,
        )

    def start(self):
        pltpu.make_async_copy(self.src, self.dst.at[self.here], self.local).start()
        for s in range(1, self.chips):
            self.far(s, self.here).start()
        self.near(0, self.core).start()

    def steps(self):
        def forward(s):
            self.far(s, self.origin(s, self.core)).wait_recv()
            self.near(s, self.core).start()

        return [partial(forward, s) for s in range(1, self.chips)]

    def finish(self):
        for s in range(self.chips):
            self.near(s, 1 - self.core).wait_recv()
            self.near(s, self.core).wait_send()
            if s:
                self.far(s, self.here).wait_send()
        pltpu.make_async_copy(self.src, self.dst.at[self.here], self.local).wait()


class LineReduce:
    def __init__(self, size, pieces, part, held, last, term, send, recv, load):
        self.size, self.pieces, self.part, self.held, self.last = size, pieces, part, held, last
        self.term, self.send, self.recv, self.load = term, send, recv, load
        self.here = lax.axis_index("tp")
        self.rows = part.shape[1] // pieces
        self.place = (self.here, size - 1 - self.here)

    def span(self, piece):
        return pl.ds(piece * self.rows, self.rows)

    def shard(self, way, hop):
        far = self.size + self.place[way] - hop
        return far if way == 0 else self.size - 1 - far

    def copy(self, way, hop, piece, first):
        rows = self.span(piece)
        source = self.part.at[self.shard(way, hop), rows] if first else self.held.at[way, hop - 2, rows]
        goal = self.last.at[way, rows] if hop == self.size - 1 else self.held.at[way, hop - 1, rows]
        return pltpu.make_async_remote_copy(
            source, goal, self.send.at[way, hop - 1, piece], self.recv.at[way, hop - 1, piece],
            device_id={"tp": self.here + (1 if way == 0 else -1)}, device_id_type=MESH,
        )

    def arrival(self, way, hop, piece):
        rows = self.span(piece)
        goal = self.last.at[way, rows] if hop == self.size - 1 else self.held.at[way, hop - 1, rows]
        return pltpu.make_async_remote_copy(
            self.part.at[0, rows], goal, self.send.at[way, hop - 1, piece], self.recv.at[way, hop - 1, piece],
            device_id={"tp": self.here}, device_id_type=MESH,
        )

    def own(self, way, hop, piece):
        return pltpu.make_async_copy(
            self.part.at[self.shard(way, hop), self.span(piece)], self.term.at[way], self.load.at[way]
        )

    def begin(self, hop, piece):
        for way in range(2):
            @pl.when(self.place[way] == 0)
            def _():
                if hop > 1:
                    self.copy(way, hop - 1, piece, True).wait_send()
                self.copy(way, hop, piece, True).start()

    def start(self):
        for piece in range(self.pieces):
            self.begin(1, piece)

    def forward(self, hop, piece):
        passes = [
            (self.place[way] > 0) & (self.place[way] < hop) & (self.place[way] < self.size - 1) for way in range(2)
        ]
        for way in range(2):
            @pl.when(passes[way])
            def _():
                self.own(way, hop, piece).start()

        self.begin(hop, piece)
        for way in range(2):
            @pl.when(passes[way])
            def _():
                self.arrival(way, hop - 1, piece).wait_recv()
                self.own(way, hop, piece).wait()
                rows = self.span(piece)
                total = self.held[way, hop - 2, rows].astype(F32) + self.term[way].astype(F32)
                self.held[way, hop - 2, rows] = total.astype(BF16)
                self.copy(way, hop, piece, False).start()

    def steps(self):
        return [
            partial(self.forward, hop, piece) for hop in range(2, self.size) for piece in range(self.pieces)
        ]

    def finish(self):
        for piece in range(self.pieces):
            for way in range(2):
                @pl.when(self.place[way] > 0)
                def _():
                    self.arrival(way, self.size - 1, piece).wait_recv()

        for hop in range(1, self.size):
            for piece in range(self.pieces):
                for way in range(2):
                    late = self.place[way] > 0 if hop < self.size - 1 else True

                    @pl.when((self.place[way] < hop) & (self.place[way] < self.size - 1) & late)
                    def _():
                        self.copy(way, hop, piece, True).wait_send()


def reduce_scratch(size, pieces, rows, width):
    dma = pltpu.SemaphoreType.DMA
    return [
        pltpu.VMEM((2, size - 2, rows, width), BF16), pltpu.VMEM((2, rows // pieces, width), BF16),
        dma((2, size - 1, pieces)), dma((2, size - 1, pieces)), dma((2,)),
    ]


class Job:
    def __init__(self, inputs, outputs, scratch, build):
        self.inputs, self.outputs, self.scratch, self.build = inputs, outputs, scratch, build


def gather_job(size, pieces, array, micro):
    _, rows, width = array.shape
    return Job(
        [array], [jax.ShapeDtypeStruct((size, rows, width), array.dtype)], gather_scratch(size, pieces),
        lambda ins, outs, scratch: LineGather(size, pieces, ins[0].at[micro], outs[0], *scratch),
    )


def landing_job(size, pieces, array, micro):
    _, rows, width = array.shape
    big = (size, rows, width)
    return Job(
        [array], [jax.ShapeDtypeStruct(big, array.dtype)], gather_scratch(size, pieces) + [
            pltpu.VMEM(big, array.dtype), pltpu.SemaphoreType.DMA((size,))
        ],
        lambda ins, outs, scratch: LineGather(size, pieces, ins[0].at[micro], scratch[3], *scratch[:3]),
    )


def reduce_job(size, pieces, side):
    slot, width = side.shape
    rows = slot // size
    return Job(
        [side.reshape(size, rows, width)], [jax.ShapeDtypeStruct((2, rows, width), BF16)],
        reduce_scratch(size, pieces, rows, width),
        lambda ins, outs, scratch: LineReduce(size, pieces, ins[0], *scratch[:1], outs[0], *scratch[1:]),
    )


def with_jobs(jobs, counts, refs):
    refs = list(refs)
    own, theirs = [], []
    for count, kind in zip(counts, ("inputs", "outputs", "scratch")):
        own += refs[:count]
        del refs[:count]
        theirs.append([])
        for job in jobs:
            many = len(getattr(job, kind))
            theirs[-1].append(refs[:many])
            del refs[:many]
    return own, [job.build(*parts) for job, parts in zip(jobs, zip(*theirs))], list(zip(*theirs))


def job_lists(jobs):
    return (
        [x for job in jobs for x in job.inputs], [x for job in jobs for x in job.outputs],
        [x for job in jobs for x in job.scratch],
    )


def spread(step, slot, slots, total, actions):
    for place in range(total // slots):
        due = [
            act for i, act in enumerate(actions)
            if (i + 1) * total // (len(actions) + 2) == place * slots + slot
        ]
        if due:
            @pl.when(step == place)
            def _():
                for act in due:
                    act()


HBM = pl.BlockSpec(memory_space=pltpu.MemorySpace.HBM)


def attention_kernel(size, jobs, row_tiles, heads, tile, *refs):
    own, lines, parts = with_jobs(jobs, (9, 3, 11), refs)
    (len_ref, x_ref, wqkv_hbm, bqkv_ref, wo_hbm, gain_ref, shift_ref, cos_ref, sin_ref, *rest) = own
    wqkv_s, wo_s, w_sem, wo_sem = rest[-4:]

    def begin():
        load_qkv = pltpu.make_async_copy(wqkv_hbm, wqkv_s, w_sem.at[0])
        load_qkv.start()
        greet([], [("tp", size)])
        for line in lines:
            line.start()
        for copy in side_by_side(wo_hbm, wo_s, wo_sem):
            copy.start()
        load_qkv.wait()

    attention_body(
        size, lines, parts, row_tiles, heads, tile, 0, begin, lambda: x_ref[...],
        lambda: [copy.wait() for copy in side_by_side(wo_hbm, wo_s, wo_sem)],
        len_ref, bqkv_ref, gain_ref, shift_ref, cos_ref, sin_ref, *rest[:-2],
    )


def opening_kernel(size, peers, pieces, counts, jobs, row_tiles, heads, tile, *refs):
    many = len(counts)
    own, lines, parts = with_jobs(jobs, (6 + many, 6 + many, 11 + 2 + 17), refs)
    len_ref, x_ref, wa_ref, wb_ref, cos_ref, sin_ref = own[:6]
    smalls, own = own[6:6 + many], own[6 + many:]
    n1_ref, att_ref, gp_ref, xs_ref, was_ref, wbs_ref = own[:6]
    outs, own = own[6:6 + many], own[6 + many:]
    work, (x_s, x_sem), more = own[:11], own[11:13], own[13:]
    send, recv, local, pack, packs, small_send, small_recv, *plane = more
    wqkv_s, wo_s, w_sem, wo_sem = work[-4:]
    here = lax.axis_index("fsdp")
    shard = xs_ref.shape[1]
    share = tile // shard

    def load_rows(at):
        slot = lax.rem(at, 2)
        return [
            pltpu.make_async_copy(
                xs_ref.at[at * share + k], x_s.at[slot, pl.ds(k * shard, shard)], x_sem.at[slot, k]
            ) for k in range(share)
        ]

    def small_copy(k, origin):
        return pltpu.make_async_remote_copy(
            pack, packs.at[origin], small_send.at[k - 1], small_recv.at[k - 1],
            device_id={"fsdp": lax.rem(here + k, peers)}, device_id_type=MESH,
        )

    def begin():
        greet([("fsdp", peers)], [("tp", size)])
        line = LineGather(size, pieces, x_ref.at[0], xs_ref, send, recv, local)
        line.start()
        weights = [PlaneGather(peers, wa_ref, was_ref, *plane[:5]), PlaneGather(peers, wb_ref, wbs_ref, *plane[5:])]
        for row, (small, count) in enumerate(zip(smalls, counts)):
            pack[row:row + 1, 0:count] = small[...].astype(F32).reshape(1, count)
        for k in range(1, peers):
            small_copy(k, here).start()
        packs[here] = pack[...]
        for weight in weights:
            weight.start()
        for act in line.steps():
            act()
        for one in lines:
            one.start()
        for weight in weights:
            for act in weight.steps():
                act()
        for k in range(1, peers):
            small_copy(k, lax.rem(here + peers - k, peers)).wait_recv()
            small_copy(k, here).wait_send()
        for row, (out, count) in enumerate(zip(outs, counts)):
            for peer in range(peers):
                out[0:1, peer * count:(peer + 1) * count] = packs[peer, row:row + 1, 0:count]
        for weight in weights:
            weight.finish()
        rows = wa_ref.shape[0]
        loads = [
            pltpu.make_async_copy(was_ref.at[k], wqkv_s.at[pl.ds(k * rows, rows)], w_sem.at[k]) for k in range(peers)
        ]
        for copy in loads + side_by_side(wbs_ref, wo_s, wo_sem):
            copy.start()
        line.finish()
        for act in lines[0].steps()[:lines[0].pieces]:
            act()
        for copy in load_rows(0):
            copy.start()
        for copy in loads:
            copy.wait()

    def rows_now():
        step = pl.program_id(0)

        @pl.when(step + 1 < row_tiles)
        def _():
            for copy in load_rows(step + 1):
                copy.start()

        for copy in load_rows(step):
            copy.wait()
        return x_s[lax.rem(step, 2)]

    attention_body(
        size, lines, parts, row_tiles, heads, tile, 1, begin, rows_now,
        lambda: [copy.wait() for copy in side_by_side(wbs_ref, wo_s, wo_sem)],
        len_ref, outs[0], outs[4], outs[5], cos_ref, sin_ref, n1_ref, att_ref, gp_ref, *work[:-2],
    )


def attention_body(
    size, lines, parts, row_tiles, heads, tile, ahead, begin, rows_now, out_ready, len_ref, bqkv_ref, gain_ref, shift_ref,
    cos_ref, sin_ref, n1_ref, att_ref, gp_ref, q_s, k_s, v_s, ga_s, p_s, dk_s, dv_s, wqkv_ref, wo_ref,
):
    cot, landed, out_sem = lines[0], parts[0][2][3], parts[0][2][4]

    def publish(shard):
        return pltpu.make_async_copy(landed.at[shard], parts[0][1][0].at[shard], out_sem.at[shard])

    step = pl.program_id(0)
    length = len_ref[0]
    scale = 1.0 / math.sqrt(HEAD)

    @pl.when(step == 0)
    def _():
        dk_s[...] = jnp.zeros_like(dk_s)
        dv_s[...] = jnp.zeros_like(dv_s)
        begin()

    @pl.when(step < row_tiles)
    def _():
        rows = pl.ds(pl.multiple_of(step * tile, tile), tile)
        xhat, _ = row_stats(rows_now().astype(F32))
        normed = (xhat * gain_ref[...] + shift_ref[...]).astype(BF16)
        n1_ref[...] = normed
        cosine, sine = cos_ref[rows, :], sin_ref[rows, :]
        for h in range(heads):
            part = dot_nn(normed, wqkv_ref[:, h * 384:(h + 1) * 384]) + bqkv_ref[:, h * 384:(h + 1) * 384]
            q, k = part[:, :HEAD], part[:, HEAD:2 * HEAD]
            q_s[h, rows, :] = (q * cosine + swap_halves(q) * sine).astype(BF16)
            k_s[h, rows, :] = (k * cosine + swap_halves(k) * sine).astype(BF16)
            v_s[h, rows, :] = part[:, 2 * HEAD:].astype(BF16)

    @pl.when((step >= row_tiles) & (step < row_tiles + heads))
    def _():
        h = step - row_tiles
        for i in range(row_tiles):
            rows, seen = slice(i * tile, (i + 1) * tile), slice(0, (i + 1) * tile)
            scores = dot_nt(q_s[h, rows, :], k_s[h, seen, :]) * scale
            place = i * tile + lax.broadcasted_iota(jnp.int32, scores.shape, 0)
            key = lax.broadcasted_iota(jnp.int32, scores.shape, 1)
            scores = jnp.where(key <= jnp.minimum(place, length - 1), scores, MASKED)
            top = jnp.max(scores, axis=-1, keepdims=True)
            raised = jnp.exp(scores - top)
            probs = (raised * (1.0 / jnp.sum(raised, axis=-1, keepdims=True))).astype(BF16)
            p_s[h, rows, seen] = probs
            att_ref[rows, :] = dot_nn(probs, v_s[h, seen, :]).astype(BF16)

    @pl.when(step == row_tiles + heads)
    def _():
        shard = landed.shape[1]
        out_ready()

        def block_back(c, h, ga):
            rows, seen = slice(c * shard, (c + 1) * shard), slice(0, (c + 1) * shard)
            probs = p_s[h, rows, seen]
            soft = probs.astype(F32)
            grad_probs = dot_nt(ga, v_s[h, seen, :])
            row_dot = jnp.sum(soft * grad_probs, axis=-1, keepdims=True)
            grad_scores = (soft * (grad_probs - row_dot)).astype(BF16)
            dq = dot_nn(grad_scores, k_s[h, seen, :]) * scale
            cosine, sine = cos_ref[rows, :], sin_ref[rows, :]
            gp_ref[rows, pl.ds(pl.multiple_of(h * 3 * HEAD, HEAD), HEAD)] = (
                dq * cosine - swap_halves(dq) * sine
            ).astype(BF16)
            dk_s[h, seen, :] += dot_tn(grad_scores, q_s[h, rows, :])
            dv_s[h, seen, :] += dot_tn(probs, ga)

        def arrive(j):
            if j == 0:
                cot.settle()
            elif j < size - 1:
                for act in cot.steps()[(j - 1) * cot.pieces:j * cot.pieces] if j > ahead else []:
                    act()
            else:
                for piece in range(cot.pieces):
                    cot.take(size - 2, piece)
            for line in lines[1:]:
                if 1 <= j < size - 1:
                    for act in line.steps()[(j - 1) * line.pieces:j * line.pieces]:
                        act()

        def one_shard(j, carry):
            for k in range(size):
                @pl.when(j == k)
                def _():
                    arrive(k)
            at = cot.order(j)
            place = at * shard + lax.broadcasted_iota(jnp.int32, landed.shape[1:], 0)
            publish(at).start()
            block = landed[at]
            ga_s[...] = dot_nt(jnp.where(place < length, block, jnp.zeros_like(block)), wo_ref[...]).astype(BF16)
            for c in range(size):
                @pl.when(at == c)
                def _():
                    def one(h, carry):
                        block_back(c, h, ga_s[:, pl.ds(pl.multiple_of(h * HEAD, HEAD), HEAD)])
                        return carry

                    lax.fori_loop(0, heads, one, 0)
            return carry

        lax.fori_loop(0, size, one_shard, 0)
        def close_head(h, carry):
            first = pl.multiple_of(h * 3 * HEAD, HEAD)
            dk = dk_s[h] * scale
            gp_ref[:, pl.ds(first + HEAD, HEAD)] = (
                dk * cos_ref[...] - swap_halves(dk) * sin_ref[...]
            ).astype(BF16)
            gp_ref[:, pl.ds(first + 2 * HEAD, HEAD)] = dv_s[h].astype(BF16)
            return carry

        lax.fori_loop(0, heads, close_head, 0)
        cot.finish(taken=True)
        for line in lines[1:]:
            line.finish()
        for k in range(size):
            publish(k).wait()


def side_by_side(parts, goal, sem):
    peers, _, width = parts.shape
    return [
        pltpu.make_async_copy(parts.at[j], goal.at[:, pl.ds(j * width, width)], sem.at[j]) for j in range(peers)
    ]


def whole(shape):
    return pl.BlockSpec(shape, lambda i: (0,) * len(shape), pipeline_mode=pl.Buffered(1))


def attention_scratch(size, slot, width, heads, peers):
    dma = pltpu.SemaphoreType.DMA
    return [pltpu.VMEM((heads, slot, HEAD), BF16)] * 3 + [
        pltpu.VMEM((slot // size, heads * HEAD), BF16), pltpu.VMEM((heads, slot, slot), BF16)
    ] + [pltpu.VMEM((heads, slot, HEAD), F32)] * 2 + [
        pltpu.VMEM((width, heads * 3 * HEAD), BF16), pltpu.VMEM((heads * HEAD, width), BF16), dma((peers,)), dma((peers,)),
    ]


def opening_call(size, peers, length, x, weights, smalls, cos, sin, jobs):
    _, rows, width = x.shape
    slot, heads = rows * size, weights[0].shape[1] // (3 * HEAD)
    tile, pieces = 256, 4
    row_tiles, chips = slot // tile, peers // 2
    counts = [small.shape[0] for small in smalls]
    pack = (-(-len(counts) // 8) * 8, -(-max(counts) // 128) * 128)
    full = pl.BlockSpec(memory_space=pltpu.VMEM)
    dma = pltpu.SemaphoreType.DMA
    row_block = pl.BlockSpec((tile, width), lambda i: (jnp.minimum(i, row_tiles - 1), 0))
    ins, outs, scratch = job_lists(jobs)
    many = len(counts)
    n1, att, gp, xs, wa, wb, *rest = pl.pallas_call(
        partial(opening_kernel, size, peers, pieces, counts, jobs, row_tiles, heads, tile),
        grid=(row_tiles + heads + 1,),
        in_specs=[pl.BlockSpec(memory_space=pltpu.SMEM), HBM, HBM, HBM, whole(cos.shape), whole(sin.shape)]
        + [full] * many + [HBM] * len(ins),
        out_specs=[
            row_block, pl.BlockSpec((slot, HEAD), lambda i: (0, jnp.clip(i - row_tiles, 0, heads - 1))),
            whole((slot, heads * 3 * HEAD)), HBM, HBM, HBM,
        ] + [whole((1, peers * count)) for count in counts] + [HBM] * len(outs),
        out_shape=[
            jax.ShapeDtypeStruct((slot, width), BF16),
            jax.ShapeDtypeStruct((slot, heads * HEAD), BF16),
            jax.ShapeDtypeStruct((slot, heads * 3 * HEAD), BF16),
            jax.ShapeDtypeStruct((size, rows, width), x.dtype),
            *(jax.ShapeDtypeStruct((peers,) + weight.shape, x.dtype) for weight in weights),
        ] + [jax.ShapeDtypeStruct((1, peers * count), F32) for count in counts] + outs,
        scratch_shapes=attention_scratch(size, slot, width, heads, peers) + [
            pltpu.VMEM((2, tile, width), BF16), dma((2, tile // rows)),
        ] + gather_scratch(size, pieces) + [
            pltpu.VMEM(pack, F32), pltpu.VMEM((peers,) + pack, F32), dma((peers - 1,)), dma((peers - 1,)),
        ] + [dma((chips,)), dma((chips,)), dma((chips,)), dma((chips,)), dma] * 2 + scratch,
        compiler_params=pltpu.CompilerParams(
            dimension_semantics=("arbitrary",), vmem_limit_bytes=VMEM_BYTES, collective_id=0, has_side_effects=True,
        ),
        cost_estimate=pl.CostEstimate(flops=int(14e9), bytes_accessed=int(400e6), transcendentals=int(3e6)),
    )(length, x, *weights, cos, sin, *smalls, *ins)
    return n1, att, gp, rest[many:], xs.reshape(slot, width), wa.reshape(width, -1), wb, rest[:many]


def attention_call(number, size, length, x, wqkv, bqkv, wo, gain, shift, cos, sin, jobs):
    slot, width = x.shape
    heads = wqkv.shape[1] // (3 * HEAD)
    tile = 256
    row_tiles = slot // tile
    row_block = pl.BlockSpec((tile, width), lambda i: (jnp.minimum(i, row_tiles - 1), 0))
    clip = lambda first: lambda i: (0, jnp.clip(i - first, 0, heads - 1))
    ins, outs, scratch = job_lists(jobs)
    n1, att, gp, *given = pl.pallas_call(
        partial(attention_kernel, size, jobs, row_tiles, heads, tile),
        grid=(row_tiles + heads + 1,),
        in_specs=[
            pl.BlockSpec(memory_space=pltpu.SMEM), row_block, HBM, whole(bqkv.shape),
            HBM, whole(gain.shape), whole(shift.shape), whole(cos.shape), whole(sin.shape),
        ] + [HBM] * len(ins),
        out_specs=[
            row_block, pl.BlockSpec((slot, HEAD), clip(row_tiles)), whole((slot, heads * 3 * HEAD)),
        ] + [HBM] * len(outs),
        out_shape=[
            jax.ShapeDtypeStruct((slot, width), BF16),
            jax.ShapeDtypeStruct((slot, heads * HEAD), BF16),
            jax.ShapeDtypeStruct((slot, heads * 3 * HEAD), BF16),
        ] + outs,
        scratch_shapes=attention_scratch(size, slot, width, heads, wo.shape[0]) + scratch,
        compiler_params=pltpu.CompilerParams(
            dimension_semantics=("arbitrary",), vmem_limit_bytes=VMEM_BYTES, collective_id=number,
            has_side_effects=True,
        ),
        cost_estimate=pl.CostEstimate(flops=int(14e9), bytes_accessed=int(20e6), transcendentals=int(3e6)),
    )(length, x, wqkv, bqkv, wo, gain, shift, cos, sin, *ins)
    return n1, att, gp, given


def normal_pair(value):
    density = jnp.exp(-0.5 * value * value)
    t = 1.0 / (1.0 + (0.3275911 * math.sqrt(0.5)) * jnp.abs(value))
    series = ((((1.061405429 * t - 1.453152027) * t) + 1.421413741) * t - 0.284496736) * t + 0.254829592
    tail = (0.5 * t) * series * density
    return jnp.where(value >= 0, 1.0 - tail, tail), density * (1.0 / math.sqrt(2.0 * math.pi))


def feed_kernel(size, jobs, tile, chunk, steps, *refs):
    own, lines, _ = with_jobs(jobs, (13, 7, 7), refs)
    step = pl.program_id(0)
    w1_hbm, w2_hbm, wo_hbm, wqkv_hbm = own[5:9]
    xhat_s, w1_s, w2_s, wo_s, wqkv_s, w_sem, part_sem = own[20:]
    loads = [
        [pltpu.make_async_copy(w1_hbm, w1_s, w_sem.at[0])], side_by_side(w2_hbm, w2_s, part_sem.at[0]),
        side_by_side(wo_hbm, wo_s, part_sem.at[1]), [pltpu.make_async_copy(wqkv_hbm, wqkv_s, w_sem.at[1])],
    ]

    @pl.when(step == 0)
    def _():
        for copy in loads[0] + loads[1]:
            copy.start()
        greet([], [("tp", size)])
        for line in lines:
            line.start()
        for copy in loads[2] + loads[3]:
            copy.start()

    def ready(which):
        @pl.when(step == 0)
        def _():
            for copy in loads[which]:
                copy.wait()

    def hook(slot):
        for line in lines:
            spread(step, slot, 4, 4 * steps, line.steps())

    feed_body(hook, ready, tile, chunk, *own[:5], w1_s, w2_s, wo_s, wqkv_s, *own[9:20], xhat_s)

    @pl.when(step == steps - 1)
    def _():
        for line in lines:
            line.finish()


def feed_body(
    hook, ready, tile, chunk, len_ref, x_ref, c_ref, att_ref, gp_ref, w1_ref, w2_ref, wo_ref, wqkv_ref, b1_ref,
    gain1_ref, gain2_ref, shift2_ref, n2_ref, act_ref, gpre_ref, h_ref, u_ref, cot_s, sd_ref, xhat_s,
):
    step = pl.program_id(0)
    length = len_ref[0]
    hidden, model = w2_ref.shape

    @pl.when(step == 0)
    def _():
        sd_ref[...] = jnp.zeros_like(sd_ref)

    xhat, _ = row_stats(x_ref[...].astype(F32))
    xhat_s[...] = xhat
    n2_ref[...] = (xhat * gain2_ref[...] + shift2_ref[...]).astype(BF16)
    place = step * tile + lax.broadcasted_iota(jnp.int32, c_ref.shape, 0)
    cot_s[...] = jnp.where(place < length, c_ref[...], jnp.zeros_like(c_ref))
    ones = jnp.ones((8, tile), BF16)
    ready(0)
    for k in range(hidden // chunk):
        cols = slice(k * chunk, (k + 1) * chunk)
        pre = dot_nn(n2_ref[...], w1_ref[:, cols]) + b1_ref[:, cols]
        below, density = normal_pair(pre)
        act_ref[:, cols] = (pre * below).astype(BF16)
        if k == 0:
            ready(1)
        gact = dot_nt(cot_s[...], w2_ref[cols, :])
        gpre = (gact * (below + pre * density)).astype(BF16)
        gpre_ref[:, cols] = gpre
        sd_ref[5:6, cols] += dot_nn(ones, gpre)[0:1]
        if k == hidden // chunk // 2 - 1:
            hook(0)
    hook(1)
    sd_ref[6:7, 0:gp_ref.shape[1]] += dot_nn(ones, gp_ref[...])[0:1]
    ready(2)
    for k in range(model // chunk):
        cols = slice(k * chunk, (k + 1) * chunk)
        h_ref[:, cols] = (
            dot_nn(act_ref[...], w2_ref[:, cols]) + dot_nn(att_ref[...], wo_ref[:, cols])
        ).astype(BF16)
    ready(3)
    hook(2)
    for k in range(model // chunk):
        cols = slice(k * chunk, (k + 1) * chunk)
        g2 = dot_nt(gpre_ref[...], w1_ref[cols, :])
        g1 = dot_nt(gp_ref[...], wqkv_ref[cols, :])
        u_ref[:, cols] = (g1 * gain1_ref[:, cols] + g2 * gain2_ref[:, cols]).astype(BF16)
        hat = xhat_s[:, cols]
        sd_ref[0:1, cols] += jnp.sum(g1 * hat, axis=0, keepdims=True)
        sd_ref[1:2, cols] += jnp.sum(g1, axis=0, keepdims=True)
        sd_ref[2:3, cols] += jnp.sum(g2 * hat, axis=0, keepdims=True)
        sd_ref[3:4, cols] += jnp.sum(g2, axis=0, keepdims=True)
        sd_ref[4:5, cols] += dot_nn(ones, cot_s[:, cols])[0:1]
    hook(3)


def feed_call(number, size, length, x, c, att, gp, w1, w2, wo, wqkv, b1, gain1, gain2, shift2, jobs):
    slot, width = x.shape
    ins, outs, scratch = job_lists(jobs)
    hidden = w1.shape[1]
    tile, chunk = 256, 512
    at = lambda i: (i, 0)
    keep = lambda i: (0, 0)
    row_block = pl.BlockSpec((tile, width), at)
    hid_block = pl.BlockSpec((tile, hidden), at)
    out = pl.pallas_call(
        partial(feed_kernel, size, jobs, tile, chunk, slot // tile),
        grid=(slot // tile,),
        in_specs=[
            pl.BlockSpec(memory_space=pltpu.SMEM), row_block, row_block, pl.BlockSpec((tile, att.shape[1]), at),
            pl.BlockSpec((tile, gp.shape[1]), at), HBM, HBM, HBM, HBM, whole(b1.shape), whole(gain1.shape), whole(gain2.shape), whole(shift2.shape),
        ] + [HBM] * len(ins),
        out_specs=[
            row_block, hid_block, hid_block, row_block, row_block, row_block, pl.BlockSpec((8, width), keep),
        ] + [HBM] * len(outs),
        out_shape=[
            jax.ShapeDtypeStruct((slot, width), BF16),
            jax.ShapeDtypeStruct((slot, hidden), BF16),
            jax.ShapeDtypeStruct((slot, hidden), BF16),
            jax.ShapeDtypeStruct((slot, width), BF16),
            jax.ShapeDtypeStruct((slot, width), BF16),
            jax.ShapeDtypeStruct((slot, width), BF16),
            jax.ShapeDtypeStruct((8, width), F32),
        ] + outs,
        scratch_shapes=[
            pltpu.VMEM((tile, width), F32), pltpu.VMEM(w1.shape, BF16), pltpu.VMEM((hidden, width), BF16),
            pltpu.VMEM((att.shape[1], width), BF16), pltpu.VMEM(wqkv.shape, BF16), pltpu.SemaphoreType.DMA((2,)),
            pltpu.SemaphoreType.DMA((2, w2.shape[0])),
        ] + scratch,
        compiler_params=pltpu.CompilerParams(
            dimension_semantics=("arbitrary",), vmem_limit_bytes=VMEM_BYTES, collective_id=number,
            has_side_effects=True,
        ),
        cost_estimate=pl.CostEstimate(flops=int(45e9), bytes_accessed=int(50e6), transcendentals=int(4e6)),
    )(length, x, c, att, gp, w1, w2, wo, wqkv, b1, gain1, gain2, shift2, *ins)
    return (*out[:7], out[7:])

LAG = 1
RING = 8


def grads_kernel(size, peers, micros, jobs, *refs):
    before = micros - 1
    own_refs, sums, _ = with_jobs(jobs, (8 * micros + 5 + 4 * before, 4 + 2 * before, 29), refs)
    take = iter(own_refs)
    lefts = [[next(take) for _ in range(micros)] for _ in range(3)]
    rights = [[next(take) for _ in range(micros)] for _ in range(4)]
    vecs = [next(take) for _ in range(micros)]
    len_ref, x_ref, c_ref, bo_ref, b2_ref = [next(take) for _ in range(5)]
    earlier = [[next(take) for _ in range(4)] for _ in range(before)]
    out_ref, turned_ref, vec_ref, vec_tp_ref = [next(take) for _ in range(4)]
    ended = [[next(take) for _ in range(2)] for _ in range(before)]
    (a_buf, b_buf, p_s, ex_send, ex_recv, out_send, recv, acc, acc_t, vec_s, vec_all, vec_line,
     a_sem, b_sem, ex_ssem, ex_rsem, out_ssem, out_rsem, w_sem, v_ssem, v_rsem, l_ssem, l_rsem,
     row_s, last_s, end_s, row_sem, last_sem, end_sem) = take
    here, line = lax.axis_index("fsdp"), lax.axis_index("tp")
    chip, core = here // 2, lax.rem(here, 2)
    chips = peers // 2
    own, wide = acc.shape[1:]
    slot = a_buf.shape[1] // micros
    chunks = acc.shape[0]
    total = chunks * chips
    firsts = [0, rights[0][0].shape[1] // wide]
    firsts.append(firsts[1] + rights[1][0].shape[1] // wide)
    firsts.append(firsts[2] + rights[2][0].shape[1] // wide)
    firsts.append(chunks)
    left_of = [0, 1, 1, 2]

    def split(unit):
        return unit // chips, lax.rem(unit, chips)

    def target(s):
        return lax.rem(chip + 1 + s, chips)

    def a_copy(group, m, unit):
        cols = pl.ds(pl.multiple_of(target(split(unit)[1]) * (2 * own), 2 * own), 2 * own)
        at = lax.rem(unit, 2)
        return pltpu.make_async_copy(
            lefts[left_of[group]][m].at[:, cols], a_buf.at[at, pl.ds(m * slot, slot)], a_sem.at[at, m]
        )

    def b_copy(group, m, chunk):
        cols = pl.ds(pl.multiple_of((chunk - firsts[group]) * wide, wide), wide)
        at = lax.rem(chunk, 2)
        return pltpu.make_async_copy(
            rights[group][m].at[:, cols], b_buf.at[at, pl.ds(m * slot, slot)], b_sem.at[at, m]
        )

    def in_group(chunk, do):
        for group in range(4):
            @pl.when((chunk >= firsts[group]) & (chunk < firsts[group + 1]))
            def _():
                for m in range(micros):
                    do(group, m)

    def exchange(unit):
        at = lax.rem(unit, RING)
        return pltpu.make_async_remote_copy(
            ex_send.at[at], ex_recv.at[at], ex_ssem.at[at], ex_rsem.at[at],
            device_id={"fsdp": 2 * chip + 1 - core}, device_id_type=MESH,
        )

    def passing(place, s):
        return pltpu.make_async_remote_copy(
            out_send.at[place], recv.at[place], out_ssem.at[place], out_rsem.at[place],
            device_id={"fsdp": 2 * target(s) + core}, device_id_type=MESH,
        )

    def process(unit):
        chunk, s = split(unit)
        exchange(unit).wait_recv()
        both = p_s[lax.rem(unit, 4), pl.ds(core * own, own), :] + ex_recv[lax.rem(unit, RING)].astype(F32)

        @pl.when(s < chips - 1)
        def _():
            place = chunk * (chips - 1) + s
            out_send[place] = both.astype(BF16)
            passing(place, s).start()

        @pl.when(s == chips - 1)
        def _():
            acc[chunk] = both

    def vec_copy(k, there):
        return pltpu.make_async_remote_copy(
            vec_s, vec_all.at[there], v_ssem.at[k - 1], v_rsem.at[k - 1],
            device_id={"fsdp": lax.rem(here + k, peers)}, device_id_type=MESH,
        )

    def line_copy(k, there):
        return pltpu.make_async_remote_copy(
            vec_ref, vec_line.at[there], l_ssem.at[k - 1], l_rsem.at[k - 1],
            device_id={"tp": lax.rem(line + k, size)}, device_id_type=MESH,
        )

    in_group(0, lambda group, m: b_copy(group, m, 0).start())
    in_group(0, lambda group, m: a_copy(group, m, 0).start())
    greet([("fsdp", peers), ("tp", size)], [])
    vec = vecs[0][...]
    for more in vecs[1:]:
        vec = vec + more[...]
    vec_s[...] = vec
    vec_all[here] = vec
    for k in range(1, peers):
        vec_copy(k, here).start()
    for one in sums:
        one.start()
    hooks = [act for acts in zip(*(one.steps() for one in sums)) for act in acts]
    span = total + 3 * chunks
    due = [(i // len(sums) + 1) * span * len(sums) // (len(hooks) + len(sums) * 2) + 2 for i in range(len(hooks))]

    def body(unit, carry):
        chunk, s = split(unit)
        after = unit + 1

        @pl.when(after < total)
        def _():
            in_group(after // chips, lambda group, m: a_copy(group, m, after).start())

        @pl.when((s == 0) & (chunk + 1 < chunks))
        def _():
            in_group(chunk + 1, lambda group, m: b_copy(group, m, chunk + 1).start())

        for m in range(micros):
            a_copy(0, m, unit).wait()

        @pl.when(s == 0)
        def _():
            for m in range(micros):
                pltpu.make_async_copy(
                    rights[0][m].at[:, pl.ds(0, wide)], b_buf.at[lax.rem(chunk, 2), pl.ds(m * slot, slot)],
                    b_sem.at[lax.rem(chunk, 2), m],
                ).wait()

        p_s[lax.rem(unit, 4)] = dot_tn(a_buf[lax.rem(unit, 2)], b_buf[lax.rem(chunk, 2)])

        @pl.when(unit >= RING)
        def _():
            exchange(unit).wait_send()

        ex_send[lax.rem(unit, RING)] = p_s[lax.rem(unit, 4), pl.ds((1 - core) * own, own), :].astype(BF16)
        exchange(unit).start()

        @pl.when(unit >= LAG)
        def _():
            process(unit - LAG)

        for i, act in enumerate(hooks):
            if due[i] < total:
                @pl.when(unit == due[i])
                def _():
                    act()

        return carry

    lax.fori_loop(0, total, body, 0)
    lax.fori_loop(total - LAG, total, lambda unit, carry: (process(unit), carry)[1], 0)

    for k in range(1, peers):
        vec_copy(k, lax.rem(here + peers - k, peers)).wait_recv()
        vec_copy(k, here).wait_send()
    vec = vec_all[0]
    for k in range(1, peers):
        vec = vec + vec_all[k]
    vec_ref[...] = vec
    vec_line[line] = vec
    for k in range(1, size):
        line_copy(k, line).start()

    step = end_s.shape[1]

    def end_step(m, k):
        at = pl.ds(k * step, step)
        h, u, h_last, u_last = earlier[m]
        loads = [
            pltpu.make_async_copy(source, row_s.at[i], row_sem.at[i])
            for i, source in enumerate((x_ref.at[m, at], c_ref.at[m, at], h.at[line, at], u.at[line, at]))
        ] + [
            pltpu.make_async_copy(source.at[:, at], last_s.at[i], last_sem.at[i])
            for i, source in enumerate((h_last, u_last))
        ]
        for copy in loads:
            copy.start()
        for copy in loads:
            copy.wait()
        local = row_s[0].astype(F32)
        place = line * x_ref.shape[1] + k * step + lax.broadcasted_iota(jnp.int32, local.shape, 0)
        y, dx = end_rows(
            local, line_total(line, size, row_s[2], last_s[0, 0], last_s[0, 1]),
            line_total(line, size, row_s[3], last_s[1, 0], last_s[1, 1]), row_s[1].astype(F32),
            place < len_ref[m, 0], bo_ref[...] + b2_ref[...],
        )
        end_s[0], end_s[1] = y, dx
        stores = [pltpu.make_async_copy(end_s.at[i], ended[m][i].at[at], end_sem.at[i]) for i in range(2)]
        for copy in stores:
            copy.start()
        for copy in stores:
            copy.wait()

    for m in range(before):
        lax.fori_loop(0, x_ref.shape[1] // step, lambda k, carry: (end_step(m, k), carry)[1], 0)

    def finish(chunk, carry):
        for i, act in enumerate(hooks):
            if due[i] >= total:
                @pl.when(chunk == min((due[i] - total) // 3, chunks - 1))
                def _():
                    act()

        value = acc[chunk]
        for s in range(chips - 1):
            place = chunk * (chips - 1) + s
            passing(place, s).wait_recv()
            value = value + recv[place].astype(F32)
        turned = (chunk >= firsts[1]) & (chunk < firsts[3])

        @pl.when(turned)
        def _():
            acc_t[chunk - firsts[1]] = value.T
            turn_out(chunk).start()

        @pl.when(jnp.logical_not(turned))
        def _():
            acc[chunk] = value
            plain_out(chunk).start()

        return carry

    def turn_out(chunk):
        at = chunk - firsts[1]
        return pltpu.make_async_copy(acc_t.at[at], turned_ref.at[at], w_sem.at[chunk])

    def plain_out(chunk):
        return pltpu.make_async_copy(acc.at[chunk], out_ref.at[chunk], w_sem.at[chunk])

    lax.fori_loop(0, chunks, finish, 0)
    for k in range(1, size):
        line_copy(k, lax.rem(line + size - k, size)).wait_recv()
        line_copy(k, line).wait_send()
    vec = vec_line[0]
    for k in range(1, size):
        vec = vec + vec_line[k]
    vec_tp_ref[...] = vec

    def close(chunk, carry):
        for s in range(chips - 1):
            passing(chunk * (chips - 1) + s, s).wait_send()
        plain_out(chunk).wait()
        return carry

    lax.fori_loop(0, chunks, close, 0)
    for one in sums:
        one.finish()
    lax.fori_loop(total - RING, total, lambda unit, carry: (exchange(unit).wait_send(), carry)[1], 0)


def grads_call(number, size, peers, lefts, rights, vecs, ends, earlier, jobs):
    micros = len(vecs)
    rows = ends[1].shape[1]
    step = min(64, rows)
    before = [x for group in earlier for x in group]
    slot, model = lefts[0][0].shape
    ins, outs, scratch = job_lists(jobs)
    own, wide = model // peers, rights[2][0].shape[1]
    chunks = sum(group[0].shape[1] for group in rights) // wide
    turned = sum(group[0].shape[1] for group in rights[1:3]) // wide
    chips = peers // 2
    full = pl.BlockSpec(memory_space=pltpu.VMEM)
    vec = jax.ShapeDtypeStruct(vecs[0].shape, F32)
    places = chunks * (chips - 1)
    dma = pltpu.SemaphoreType.DMA
    flat = [x for group in (*lefts, *rights) for x in group]
    return pl.pallas_call(
        partial(grads_kernel, size, peers, micros, jobs),
        in_specs=[HBM] * len(flat) + [full] * micros + [
            pl.BlockSpec(memory_space=pltpu.SMEM), HBM, HBM, full, full
        ] + [HBM] * len(before) + [HBM] * len(ins),
        out_specs=[HBM, HBM, full, full] + [HBM] * (2 * len(earlier)) + [HBM] * len(outs),
        out_shape=[
            jax.ShapeDtypeStruct((chunks, own, wide), F32), jax.ShapeDtypeStruct((turned, wide, own), F32), vec, vec
        ]
        + [jax.ShapeDtypeStruct((rows, model), BF16)] * (2 * len(earlier)) + outs,
        scratch_shapes=[
            pltpu.VMEM((2, micros * slot, 2 * own), BF16), pltpu.VMEM((2, micros * slot, wide), BF16),
            pltpu.VMEM((4, 2 * own, wide), F32), pltpu.VMEM((RING, own, wide), BF16),
            pltpu.VMEM((RING, own, wide), BF16), pltpu.VMEM((places, own, wide), BF16),
            pltpu.VMEM((places, own, wide), BF16), pltpu.VMEM((chunks, own, wide), F32),
            pltpu.VMEM((turned, wide, own), F32),
            pltpu.VMEM(vec.shape, F32), pltpu.VMEM((peers,) + vec.shape, F32), pltpu.VMEM((size,) + vec.shape, F32),
            dma((2, micros)), dma((2, micros)), dma((RING,)), dma((RING,)), dma((places,)), dma((places,)),
            dma((chunks,)), dma((peers - 1,)), dma((peers - 1,)), dma((size - 1,)), dma((size - 1,)),
            pltpu.VMEM((4, step, model), BF16), pltpu.VMEM((2, 2, step, model), BF16),
            pltpu.VMEM((2, step, model), BF16), dma((4,)), dma((2,)), dma((2,)),
        ] + scratch,
        compiler_params=pltpu.CompilerParams(
            collective_id=number, has_side_effects=True, vmem_limit_bytes=VMEM_BYTES
        ),
        cost_estimate=pl.CostEstimate(flops=int(52e9), bytes_accessed=int(200e6), transcendentals=0),
    )(*flat, *vecs, *ends, *before, *ins)


def end_rows(local, h, u, cot, live, shift):
    xhat, rstd = row_stats(local)
    back = rstd * (u - jnp.mean(u, axis=-1, keepdims=True) - xhat * jnp.mean(u * xhat, axis=-1, keepdims=True))
    return (
        jnp.where(live, local + h + shift, 0.0).astype(BF16), (jnp.where(live, cot, 0.0) + back).astype(BF16),
    )


def line_total(here, size, own, left, right):
    value = own.astype(F32) + jnp.where(here > 0, left.astype(F32), 0.0)
    return value + jnp.where(here < size - 1, right.astype(F32), 0.0)


def close_kernel(
    size, hidden, peers, micros, len_ref, x_ref, c_ref, bo_ref, b2_ref, vec_ref, vec_tp_ref, g_ref, turned_ref, *refs,
):
    before = micros - 1
    h_ref, u_ref, h_last, u_last = refs[:4]
    ended, refs = refs[4:4 + 2 * before], refs[4 + 2 * before:]
    y_ref, dx_ref, up_ref, down_ref, out_ref, qkv_ref = refs[:6]
    rows_out = refs[6:14]
    row_s, last_s, g_s, t_s, row_sem, g_sem, done_sem = refs[14:]
    here = lax.axis_index("tp")
    chunks, own, wide = g_ref.shape
    dma = pltpu.make_async_copy
    plain = [*range(hidden), *range(2 * hidden + 1, chunks)]
    arrive = [dma(g_ref.at[b], g_s.at[i], g_sem.at[b]) for i, b in enumerate(plain)]
    arrive += [dma(turned_ref.at[b], t_s.at[b], g_sem.at[hidden + b]) for b in range(hidden + 1)]
    loads = [
        dma(source, row_s.at[i], row_sem.at[i])
        for i, source in enumerate((x_ref.at[before], c_ref.at[before], h_ref.at[here], u_ref.at[here]))
    ] + [dma(source, last_s.at[i], row_sem.at[4 + i]) for i, source in enumerate((h_last, u_last))]
    copies = [
        dma(ended[2 * m + k], (y_ref, dx_ref)[k].at[m], done_sem.at[2 * m + k]) for m in range(before) for k in range(2)
    ]
    for copy in arrive + loads + copies:
        copy.start()
    sources = [(vec_tp_ref, k) for k in range(4)] + [(vec_ref, k) for k in (4, 4, 5, 6)]
    for peer in range(peers):
        @pl.when(lax.axis_index("fsdp") == peer)
        def _():
            for goal, (source, row) in zip(rows_out, sources):
                count = goal.shape[0]
                goal[...] = source[row:row + 1, peer * count:(peer + 1) * count].reshape(count)

    rows = row_s.shape[1]
    step = min(64, rows)

    def end_step(k, carry):
        at = pl.ds(k * step, step)
        local = row_s[0, at].astype(F32)
        place = here * rows + k * step + lax.broadcasted_iota(jnp.int32, local.shape, 0)
        y_ref[before, at], dx_ref[before, at] = end_rows(
            local, line_total(here, size, row_s[2, at], last_s[0, 0, at], last_s[0, 1, at]),
            line_total(here, size, row_s[3, at], last_s[1, 0, at], last_s[1, 1, at]), row_s[1, at].astype(F32),
            place < len_ref[before, 0], bo_ref[...] + b2_ref[...],
        )
        return carry

    ends = []
    for i, b in enumerate(plain):
        goal, at = (up_ref, b) if b < hidden else (qkv_ref, b - 2 * hidden - 1)
        ends.append(dma(g_s.at[i], goal.at[:, pl.ds(at * wide, wide)], g_sem.at[b]))
    for b in range(hidden + 1):
        goal = down_ref.at[pl.ds(b * wide, wide)] if b < hidden else out_ref
        ends.append(dma(t_s.at[b], goal, g_sem.at[hidden + b]))
    for came, leaves in zip(arrive, ends):
        came.wait()
        leaves.start()
    for copy in loads:
        copy.wait()
    lax.fori_loop(0, rows // step, end_step, 0)
    for copy in copies + ends:
        copy.wait()


def close_call(size, peers, lengths, x, c, bo, b2, vec, vec_tp, grads, turned, sides, lasts, ended, counts):
    micros, rows, width = x.shape
    chunks, own, wide = grads.shape
    hidden = (chunks - 4) // 2
    full = pl.BlockSpec(memory_space=pltpu.VMEM)
    dma = pltpu.SemaphoreType.DMA
    return pl.pallas_call(
        partial(close_kernel, size, hidden, peers, micros),
        in_specs=[pl.BlockSpec(memory_space=pltpu.SMEM), HBM, HBM, full, full, full, full, HBM, HBM]
        + [HBM] * (4 + len(ended)),
        out_specs=[full, full, HBM, HBM, HBM, HBM] + [full] * 8,
        out_shape=[
            jax.ShapeDtypeStruct(x.shape, BF16), jax.ShapeDtypeStruct(x.shape, BF16),
            jax.ShapeDtypeStruct((own, hidden * wide), F32), jax.ShapeDtypeStruct((hidden * wide, own), F32),
            jax.ShapeDtypeStruct((wide, own), F32), jax.ShapeDtypeStruct((own, 3 * wide), F32),
        ] + [jax.ShapeDtypeStruct((count,), F32) for count in counts],
        scratch_shapes=[
            pltpu.VMEM((4, rows, width), BF16), pltpu.VMEM((2, 2, rows, width), BF16),
            pltpu.VMEM((hidden + 3, own, wide), F32), pltpu.VMEM((hidden + 1, wide, own), F32),
            dma((6,)), dma((chunks,)), dma((max(len(ended), 1),)),
        ],
        compiler_params=pltpu.CompilerParams(vmem_limit_bytes=VMEM_BYTES),
        cost_estimate=pl.CostEstimate(flops=0, bytes_accessed=int(36e6), transcendentals=0),
    )(lengths, x, c, bo, b2, vec, vec_tp, grads, turned, *sides, *lasts, *ended)


def shards(
    hidden_in, out_grad, lengths, qkv_weight, qkv_bias, out_weight, out_bias, fc1_weight, fc1_bias,
    fc2_weight, fc2_bias, ln1_gain, ln1_bias, ln2_gain, ln2_bias,
):
    tp_size = lax.axis_size("tp")
    fsdp_index = lax.axis_index("fsdp")
    micro_count, shard_rows, model = hidden_in.shape
    slot = shard_rows * tp_size
    own = out_bias.shape[0]
    cos, sin = rotary_full(slot)
    gather = lambda value, axis: lax.all_gather(value, axis, axis=0, tiled=True)

    small = (qkv_bias, fc1_bias, out_bias, fc2_bias, ln1_gain, ln1_bias, ln2_gain, ln2_bias)
    peers = lax.axis_size("fsdp")
    w1 = gather(fc1_weight, "fsdp")
    w2 = lax.all_gather(fc2_weight, "fsdp", axis=0, tiled=False)

    parts, sides, lasts = [], [], []
    for m in range(micro_count):
        length = lengths[m]
        jobs = [landing_job(tp_size, 2, out_grad, m)]
        if m:
            jobs.append(reduce_job(tp_size, 2, sides[m - 1][0]))
        if m == 0:
            n1, att, gp, (c, *last), x, wqkv, wo, vectors = opening_call(
                tp_size, peers, length, hidden_in, (qkv_weight, out_weight), small, cos, sin, jobs
            )
            bqkv, b1, bo, b2, gain1, shift1, gain2, shift2 = vectors
        else:
            n1, att, gp, (c, *last) = attention_call(
                1 + 2 * m, tp_size, length, x, wqkv, bqkv, wo, gain1, shift1, cos, sin, jobs
            )
        jobs = [reduce_job(tp_size, 2, sides[m - 1][1])] if m else []
        if m + 1 < micro_count:
            jobs.append(gather_job(tp_size, 2, hidden_in, m + 1))
        n2, act, gpre, h, u, cot, sums, given = feed_call(
            2 + 2 * m, tp_size, length, x, c.reshape(slot, model), att, gp, w1, w2, wo, wqkv, b1, gain1, gain2,
            shift2, jobs,
        )
        if m:
            lasts.append((*last, given[0]))
        parts.append((n2, cot, n1, gpre, act, att, gp, sums))
        sides.append((h, u))
        if m + 1 < micro_count:
            x = given[-1].reshape(slot, model)

    by_kind = [list(kind) for kind in zip(*parts)]
    sides = [[side.reshape(tp_size, shard_rows, model) for side in pair] for pair in sides]
    grads, turned, vec, vec_tp, *rest = grads_call(
        1 + 2 * micro_count, tp_size, peers, by_kind[0:3], by_kind[3:7], by_kind[7],
        (lengths, hidden_in, out_grad, bo, b2), [(*side, *last) for side, last in zip(sides, lasts)],
        [reduce_job(tp_size, 2, side.reshape(slot, model)) for side in sides[-1]],
    )
    ended, last = rest[:-2], rest[-2:]
    y, dx, grad_up, grad_down, grad_out, grad_qkv, *rows = close_call(
        tp_size, peers, lengths, hidden_in, out_grad, bo, b2, vec, vec_tp, grads, turned, sides[-1], last, ended,
        [own] * 6 + [fc1_bias.shape[0], qkv_bias.shape[0]],
    )
    ln, grad_bias, grad_bias_two, grad_b1, grad_bq = rows[:4], *rows[4:]
    return (
        y, dx, grad_qkv, grad_bq, grad_out, grad_bias, grad_up, grad_b1,
        grad_down, grad_bias_two, ln[0], ln[1], ln[2], ln[3],
    )


def solution(mesh):
    rows = P(None, ("fsdp", "tp"), None)
    both, column, row, one = P(("tp", "fsdp")), P("fsdp", "tp"), P("tp", "fsdp"), P("fsdp")
    return jax.shard_map(
        shards,
        mesh=mesh,
        in_specs=(rows, rows, P(None, "fsdp"), column, both, row, one, column, both, row, one, one, one, one, one),
        out_specs=(rows, rows, column, both, row, one, column, both, row, one, one, one, one, one),
        check_vma=False,
    )
```

time: 985 us -> 593 us (0.60)
  waiting for transfers between devices: 363 us -> 1.42 us
  Pallas kernels: 431 us -> 566 us
  matrix products: 96.2 us -> 0 us
  blocking collectives: 35.7 us -> 0 us
  other arithmetic: 27.1 us -> 0 us
  local copies, waits for them, and re-layouts: 12.8 us -> 2.62 us
    reduce_scatter x8 -> x0, waiting for transfers between devices: 359 us -> none  [the longest x4 201 us: weight_grad(): lax.psum_scatter(total.astype(BF16), 'fsdp', scatter_dimension=0, tiled=T...]
    pallas_call x5 -> x6, Pallas kernels: 431 us -> 566 us  [the longest x1 153 us: opening_call(): pl.pallas_call(partial(opening_kernel, size, peers, pieces, counts, jobs,...]
    dot_general x8 -> x0, matrix products: 96.2 us -> none  [dot_tn(): lax.dot_general(a, b, (((0,), (0,)), ((), ())), preferred_element_type=F32)]
    psum x2 -> x0, blocking collectives: 35.7 us -> none  [the longest x1 24.3 us: shards(): lax.psum(jnp.concatenate([sums[0][:5].reshape(-1), sums[1][0], sums[2][0]...]
  transfers between devices with their start and end apart: 12 -> 2, of which waited for: 5 -> 0; matrix products, arithmetic and copies ran while one was open for 13% -> 0% of each run, Pallas kernels for 31% -> 26%
where the time goes in v3:
time: 593 us; the launch traced here: 585 us
  Pallas kernels  566 us (95%)
  between operations  14.6 us (2%)
    pallas_call x1, Pallas kernels, opening_call(): pl.pallas_call(partial(opening_kernel, size, peers, pieces, counts, jobs,...  153 us
    pallas_call x2, Pallas kernels, feed_call(): pl.pallas_call(partial(feed_kernel, size, jobs, tile, chunk, slot // tile...  149 us
    pallas_call x1, Pallas kernels, grads_call(): pl.pallas_call(partial(grads_kernel, size, peers, micros, jobs), in_specs...  148 us
    pallas_call x1, Pallas kernels, attention_call(): pl.pallas_call(partial(attention_kernel, size, jobs, row_tiles, heads, ti...  100 us
    pallas_call x1, Pallas kernels, close_call(): pl.pallas_call(partial(close_kernel, size, hidden, peers, micros), in_spe...  14.9 us
  transfers between devices with their start and end apart: 2, of which 0 were waited for; matrix products, arithmetic and copies ran while one was open for 0% of the time, Pallas kernels for 26%

profile of v3, /device:TPU:0, one launch (start us, length us, event | category | flops | bytes accessed | tf_op | source)
XLA Modules:
  0.0 584.7 jit_solution(6073342603351696349)
XLA Ops:
  7.2 0.0 all-gather.4.cloned.1.call-start
  7.2 0.7 all-gather.4.cloned.1.call-update
  7.9 0.0 all-gather.6.cloned.1.call-start
  8.0 0.7 all-gather.6.cloned.1.call-update
  8.7 1.3 copy.32.refs_16_.len_ref
  10.0 1.3 fusion
  11.3 153.2 %shard_map.272 = (bf16[1024,2048]{1,0:T(8,128)(2,1)}, bf16[1024,512]{1,0:T(8,128)(2,1)}, bf16[1024,1536]{1,0:T(8,128)(2,1)}, bf16[4,256,2048]{2,1,0:T(8,128)(2,1...) custom-call(s32[1]{0:T(128)} %bitcast.refs_0_, ...), custom_call_target="tpu_custom_call" | custom-call | flops 14000000000 | bytes 400000000 | tf_op jit(solution)/shard_map/pallas_call | solution.py:652
  164.5 0.0 all-gather.4.cloned.1.call-done.refs_5_
  164.5 0.0 all-gather.6.cloned.1.call-done
  164.5 76.4 %shard_map.273 = (bf16[1024,2048]{1,0:T(8,128)(2,1)}, bf16[1024,2048]{1,0:T(8,128)(2,1)}, bf16[1024,2048]{1,0:T(8,128)(2,1)}, bf16[1024,2048]{1,0:T(8,128)(2,1)}...) custom-call(s32[1]{0:T(128)} %bitcast.refs_0_, ...), custom_call_target="tpu_custom_call" | custom-call | flops 44999999488 | bytes 50000000 | tf_op jit(solution)/shard_map/pallas_call | solution.py:825
  240.9 100.3 %shard_map.274 = (bf16[1024,2048]{1,0:T(8,128)(2,1)}, bf16[1024,512]{1,0:T(8,128)(2,1)}, bf16[1024,1536]{1,0:T(8,128)(2,1)}, bf16[4,256,2048]{2,1,0:T(8,128)(2,1)}, bf16[2,256,2048]{2,1,0:T(8,128)(2,1)}) custom-call(s32[1]{0:T(128)} %bitcast.5.refs_0_, bf16[1024,2048]{1,0:T(8,128)(2,1)} %bitcast.25, bf16[2048,1536]{1,0:T(8,128)(2,1)} %bitcast.19, ...), custom_call_target="tpu_custom_call" | custom-call | flops 14000000000 | bytes 20000000 | tf_op jit(solution)/shard_map/pallas_call | solution.py:689
  341.2 73.0 %shard_map.275 = (bf16[1024,2048]{1,0:T(8,128)(2,1)}, bf16[1024,2048]{1,0:T(8,128)(2,1)}, bf16[1024,2048]{1,0:T(8,128)(2,1)}, bf16[1024,2048]{1,0:T(8,128)(2,1)}...) custom-call(s32[1]{0:T(128)} %bitcast.5.refs_0_, ...), custom_call_target="tpu_custom_call" | custom-call | flops 44999999488 | bytes 50000000 | tf_op jit(solution)/shard_map/pallas_call | solution.py:825
  414.2 148.3 %shard_map.276 = (f32[12,256,512]{2,1,0:T(8,128)}, f32[5,512,256]{2,1,0:T(8,128)}, f32[8,2048]{1,0:T(8,128)}, f32[8,2048]{1,0:T(8,128)}, bf16[256,2048]{1,0:T(8,...) custom-call(bf16[1024,2048]{1,0:T(8,128)(2,1)} %get-tuple-element.84.refs_0_, ...), custom_call_target="tpu_custom_call" | custom-call | flops 51999997952 | bytes 200000000 | tf_op jit(solution)/shard_map/pallas_call | solution.py:1132
  562.5 14.9 %shard_map.277 = (bf16[2,256,2048]{2,1,0:T(8,128)(2,1)}, bf16[2,256,2048]{2,1,0:T(8,128)(2,1)}, f32[256,2048]{1,0:T(8,128)}, f32[2048,256]{1,0:T(8,128)}, f32[51...) custom-call(s32[2,1]{1,0:T(2,128)} %copy.32.refs_16_.len_ref, ...), custom_call_target="tpu_custom_call" | custom-call | bytes 36000000 | tf_op jit(solution)/shard_map/pallas_call | solution.py:1243
Async XLA Ops:
  7.2 157.3 %all-gather.4.cloned.1.call-start = ((), (), s32[]{:S(2)}) async-start(), calls=%async_computation | async-start | bytes 9437184 | tf_op jit(solution)/shard_map/all_gather | solution.py:1273
  7.9 156.6 %all-gather.6.cloned.1.call-start = ((), (), s32[]{:S(2)}) async-start(), calls=%async_computation.1 | async-start | bytes 9437184 | tf_op jit(solution)/shard_map/all_gather | solution.py:1278
Sparse Core Ops, SparseCore 0:
  9.9 90.6 all-gather.3
  102.5 54.6 all-gather.5
